TPU v7x, 32 devices: a whole 2x2x4 slice. The times are simulated.
32 devices in a mesh: rows: 8 (over y, x, core), tp: 4 (over z).
Axes of the slice: x: 2, y: 2, z: 4, core: 2. Of those that a mesh axis runs over, the one named last changes fastest.
Arguments:
- features: bfloat16 [16384, 768], P('rows'), may hold values from -6 to 6
- type_ids: int32 [16384], P('rows'), may hold values 0 or 1
- segment_ids: int32 [32, 512], P('rows'), may hold values from 0 to 3, never falling along the last dimension, each value on 1 to 256 neighbouring positions
- type_table: bfloat16 [2, 768], replicated, may hold values from -3 to 3
- w_qkv: bfloat16 [3, 768, 768], P(None, None, 'tp'), may hold values from -0.3125 to 0.3125
- b_qv: bfloat16 [2, 768], P(None, 'tp'), may hold values from -3 to 3
- w_out: bfloat16 [768, 768], P('tp'), may hold values from -0.875 to 0.875
- b_out: bfloat16 [768], replicated, may hold values from -3 to 3
- gain_attn: bfloat16 [768], replicated, may hold values from 0.25 to 1.75
- shift_attn: bfloat16 [768], replicated, may hold values from -3 to 3
- w_up: bfloat16 [768, 3072], P(None, 'tp'), may hold values from -0.21875 to 0.21875
- b_up: bfloat16 [3072], P('tp'), may hold values from -3 to 3
- w_down: bfloat16 [3072, 768], P('tp'), may hold values from -0.109375 to 0.109375
- b_down: bfloat16 [768], replicated, may hold values from -3 to 3
- gain_ffn: bfloat16 [768], replicated, may hold values from 0.25 to 1.75
- shift_ffn: bfloat16 [768], replicated, may hold values from -3 to 3
- cotangent: bfloat16 [16384, 768], P('rows'), may hold values from -6 to 6
Outputs:
- output: bfloat16 [16384, 768], P('rows')
- grad_features: bfloat16 [16384, 768], P('rows')
- grad_table: float32 [2, 768], replicated
- grad_qkv: float32 [3, 768, 768], P(None, None, 'tp')
- grad_bias_qv: float32 [2, 768], P(None, 'tp')
- grad_w_out: float32 [768, 768], P('tp')
- grad_b_out: float32 [768], replicated
- grad_gain_attn: float32 [768], replicated
- grad_shift_attn: float32 [768], replicated
- grad_w_up: float32 [768, 3072], P(None, 'tp')
- grad_b_up: float32 [3072], P('tp')
- grad_w_down: float32 [3072, 768], P('tp')
- grad_b_down: float32 [768], replicated
- grad_gain_ffn: float32 [768], replicated
- grad_shift_ffn: float32 [768], replicated
Inputs may be any that keep to these rules, and one draw needn't show every extreme that they name: `segment_ids`: along each packed row the ids never fall; each of the 4 ids covers 1 to 256 tokens, and one covers exactly 256.
All inputs are finite; a program needn't handle non-finite values. No bound on the sum of `type_ids` on one device may be relied on, other than what follows from the above.
Results may differ from a plain program's by a relative error of at most 0.015.
The roundings to bfloat16 on the way count: a program that leaves them out, or rounds other values in their place, can miss the bound.
Values sent between devices are 32-bit elements; how exact they have to be, the bound alone decides.
No kernel may reach another device: no remote copies, remote signals or barrier semaphores. Data moves between devices by JAX's collectives and lax.ppermute only.
A program may use at most 128 MiB of HBM per device.

v0:
```python
from functools import partial

import jax
import jax.numpy as jnp
from jax import lax
from jax.experimental import pallas as pl
from jax.experimental.pallas import tpu as pltpu
from jax.sharding import PartitionSpec as P


HEAD_DIM = 64
BITS = 3
PIECES = 1 << BITS
NEG = -1000000000.0


def normalize(hidden):
    center = hidden - jnp.mean(hidden, axis=-1, keepdims=True)
    variance = jnp.mean(center * center, axis=-1, keepdims=True)
    inverse = lax.rsqrt(variance + 1e-05)
    return (center * inverse, inverse)


def norm_back(grad_norm, normed, inverse):
    mean_grad = jnp.mean(grad_norm, axis=-1, keepdims=True)
    mean_proj = jnp.mean(grad_norm * normed, axis=-1, keepdims=True)
    return inverse * (grad_norm - mean_grad - normed * mean_proj)


def f32(x):
    return x.astype(jnp.float32)


def bf16(x):
    return x.astype(jnp.bfloat16)


def round_kernel(x_ref, *refs):
    refs[-1][...] = x_ref[...].astype(jnp.bfloat16)


def rounded(x, *deps):
    n, d = x.shape
    block = n // 4
    return pl.pallas_call(
        round_kernel,
        grid=(4,),
        in_specs=[pl.BlockSpec((block, d), lambda i: (i, 0))]
        + [pl.BlockSpec(memory_space=pl.ANY)] * len(deps),
        out_specs=pl.BlockSpec((block, d), lambda i: (i, 0)),
        out_shape=jax.ShapeDtypeStruct((n, d), jnp.bfloat16),
    )(x, *deps)


def pack_kernel(*refs):
    row = 0
    for ref in refs[:-1]:
        refs[-1][row : row + ref.shape[0], :] = ref[...]
        row += ref.shape[0]


def pack(parts, d):
    parts = [x.reshape(-1, d) for x in parts]
    rows = sum(x.shape[0] for x in parts)
    return pl.pallas_call(
        pack_kernel,
        in_specs=[pl.BlockSpec(memory_space=pltpu.VMEM)] * len(parts),
        out_specs=pl.BlockSpec(memory_space=pltpu.VMEM),
        out_shape=jax.ShapeDtypeStruct((rows, d), jnp.float32),
    )(*parts)


def bias_kernel(scalars_ref, *refs, tp, heads, inward):
    z = scalars_ref[2]
    quads = PIECES // 2
    for t in range(tp):
        a = (z + tp - t) % tp
        shard = z ^ a if inward else a

        def move(x_ref, o_ref, there, here):
            if inward:
                there, here = here, there
            o_ref[pl.ds(there, 1), :] = x_ref[pl.ds(here, 1), :]

        for i in range(PIECES):
            for n in (0, 1):
                for h in range(heads):
                    there = (shard * heads + h) * PIECES + (i ^ scalars_ref[n])
                    move(refs[n], refs[n + 3], there, (t * heads + h) * PIECES + i)
                there = (shard * 2 + n) * PIECES + (i ^ scalars_ref[n])
                row = (((i // quads) * 2 + n) * quads + i % quads) * tp + t
                move(refs[2], refs[5], there, row)


def bias_rows(scalars, q, v, f, tp, heads, inward):
    return pl.pallas_call(
        partial(bias_kernel, tp=tp, heads=heads, inward=inward),
        in_specs=[pl.BlockSpec(memory_space=pltpu.SMEM)]
        + [pl.BlockSpec(memory_space=pltpu.VMEM)] * 3,
        out_specs=[pl.BlockSpec(memory_space=pltpu.VMEM)] * 3,
        out_shape=[jax.ShapeDtypeStruct(x.shape, x.dtype) for x in (q, v, f)],
    )(scalars, q, v, f)


def join_ffn_kernel(masks_ref, own_ref, mine_ref, other_ref, o_ref):
    mask = masks_ref[pl.program_id(0)]
    quads = mine_ref.shape[1]
    for i in range(2 * quads):
        o_ref[i // quads, 0, i % quads, 0] = own_ref[0, i ^ mask]
    o_ref[0, 0, :, 1:] = mine_ref[0, :, :, 0].astype(jnp.bfloat16)
    o_ref[1, 0, :, 1:] = other_ref[0, :, :, 0].astype(jnp.bfloat16)


def join_ffn(masks, own, mine, other, which):
    _, quads, others, _, n, d = mine.shape
    spec = pl.BlockSpec((1, quads, others, 1, n, d), lambda s, m: (s, 0, 0, which, 0, 0))
    return pl.pallas_call(
        join_ffn_kernel,
        grid_spec=pltpu.PrefetchScalarGridSpec(
            num_scalar_prefetch=1,
            grid=(2,),
            in_specs=[
                pl.BlockSpec((1, 2 * quads, n, d), lambda s, m: (s, 0, 0, 0)),
                spec,
                spec,
            ],
            out_specs=pl.BlockSpec(
                (2, 1, quads, others + 1, n, d), lambda s, m: (0, s, 0, 0, 0, 0)
            ),
        ),
        out_shape=jax.ShapeDtypeStruct((2, 2, quads, others + 1, n, d), jnp.bfloat16),
    )(masks, own, mine, other)


def join_att_kernel(masks_ref, own_ref, mine_ref, other_ref, o_ref):
    mask = masks_ref[pl.program_id(0)]
    _, _, heads, pieces, _, _ = own_ref.shape
    quads, others = mine_ref.shape[1:3]
    for h in range(heads):
        parts = [own_ref[0, 0, h, j ^ mask] for j in range(pieces)]
        o_ref[0, 0, 0, h] = jnp.concatenate(parts).astype(jnp.bfloat16)
        for t in range(others):
            parts = [ref[0, j, t, 0, h] for ref in (mine_ref, other_ref) for j in range(quads)]
            o_ref[0, 0, t + 1, h] = jnp.concatenate(parts).astype(jnp.bfloat16)


def join_att(masks, own, mine, other):
    _, quads, others, _, heads, e, d = mine.shape
    pieces = own.shape[3]
    spec = pl.BlockSpec((1, quads, others, 1, heads, e, d), lambda s, i, m: (s, 0, 0, i, 0, 0, 0))
    return pl.pallas_call(
        join_att_kernel,
        grid_spec=pltpu.PrefetchScalarGridSpec(
            num_scalar_prefetch=1,
            grid=(2, 2),
            in_specs=[
                pl.BlockSpec((1, 1, heads, pieces, e, d), lambda s, i, m: (s, i, 0, 0, 0, 0)),
                spec,
                spec,
            ],
            out_specs=pl.BlockSpec(
                (1, 1, others + 1, heads, pieces * e, d), lambda s, i, m: (s, i, 0, 0, 0, 0)
            ),
        ),
        out_shape=jax.ShapeDtypeStruct((2, 2, others + 1, heads, pieces * e, d), jnp.bfloat16),
    )(masks, own, mine, other)


def place_kernel(masks_ref, mine_ref, other_ref, o_ref):
    mask = masks_ref[pl.program_id(0)]
    quads = mine_ref.shape[1]
    for i in range(2 * quads):
        j = i ^ mask
        low = mine_ref[0, j & (quads - 1)]
        high = other_ref[0, j & (quads - 1)]
        o_ref[0, i] = jnp.where(j < quads, low, high)


def place(masks, mine, other):
    _, quads, n, d = mine.shape
    spec = pl.BlockSpec((1, quads, n, d), lambda s, m: (s, 0, 0, 0))
    return pl.pallas_call(
        place_kernel,
        grid_spec=pltpu.PrefetchScalarGridSpec(
            num_scalar_prefetch=1,
            grid=(2,),
            in_specs=[spec, spec],
            out_specs=pl.BlockSpec((1, 2 * quads, n, d), lambda s, m: (s, 0, 0, 0)),
        ),
        out_shape=jax.ShapeDtypeStruct((2, 2 * quads, n, d), jnp.float32),
    )(masks, mine, other)


def dot_t(a, b):
    return lax.dot_general(a, b, (((1,), (1,)), ((), ())), preferred_element_type=jnp.float32)


def dot_n(a, b):
    return lax.dot_general(a, b, (((1,), (0,)), ((), ())), preferred_element_type=jnp.float32)


def dot_a(a, b):
    return lax.dot_general(a, b, (((0,), (0,)), ((), ())), preferred_element_type=jnp.float32)


def make(mesh):
    rows = mesh.shape["rows"]
    T = mesh.shape["tp"]
    row_bits = rows.bit_length() - 1
    tp_bits = [1 << b for b in range(T.bit_length() - 1)]

    def swap(x, bit):
        return lax.ppermute(x, "rows", [(i, i ^ (1 << bit)) for i in range(rows)])

    def shift(x, k):
        return lax.ppermute(x, "tp", [(i, (i + k) % T) for i in range(T)])

    def shards(piece):
        others = [shift(piece, k) for k in range(1, T)]
        return [jnp.stack([x[s] for x in others]) for s in (0, 1)]

    def swap_first(bufs):
        return [jnp.stack([b, swap(b, bit)]) for b, bit in zip(bufs, (1, 2))]

    def swap_second(bufs):
        return jnp.stack([jnp.stack([b, swap(b, bit)]) for b, bit in zip(bufs, (2, 1))])

    def total_over(x):
        for bit in range(row_bits):
            x = x + swap(x, bit)
        for m in tp_bits:
            x = x + lax.ppermute(x, "tp", [(i, i ^ m) for i in range(T)])
        return x

    def halve_core(keep, send):
        return keep + swap(send, 0)

    def halve_first(both):
        return [both[s][0] + swap(both[s][1], bit) for s, bit in ((0, 2), (1, 1))]

    def halve_second(accs):
        return [acc[0] + swap(acc[1], bit) for acc, bit in zip(accs, (1, 2))]

    def shard_sum(accs):
        acc = jnp.stack(accs, axis=1)
        total = acc[0] + sum(shift(acc[T - k], k) for k in range(1, T))
        for bit in range(BITS, row_bits):
            total = total + swap(total, bit)
        return total

    def spread(total):
        both = swap_second(swap_first([total[0], total[1]]))
        both = both.reshape(2, PIECES // 2, total.shape[1], total.shape[2])
        return both, swap(both, 0)

    def per_device(
        features, type_ids, segment_ids, type_table, w_qkv, b_qv, w_out, b_out, gain_attn,
        shift_attn, w_up, b_up, w_down, b_down, gain_ffn, shift_ffn, cotangent,
    ):
        z = lax.axis_index("tp")
        r = lax.axis_index("rows")
        bits = [(r >> b) & 1 for b in range(BITS)]
        mask_a = bits[0] * 4 + bits[2] * 2 + bits[1]
        mask_b = bits[0] * 4 + bits[1] * 2 + bits[2]
        masks = (mask_a, mask_b)
        D = features.shape[1]
        width = w_qkv.shape[2]
        heads = width // HEAD_DIM
        shard_ff = w_up.shape[1]
        tokens = features.shape[0] // T
        length = segment_ids.shape[1]
        nrows = segment_ids.shape[0] // T
        E = HEAD_DIM // PIECES
        FP = shard_ff // (2 * PIECES)

        def own_slice(x, n):
            return lax.dynamic_slice_in_dim(x, z * n, n, 0)

        def pick(x, mask, axis):
            return lax.dynamic_index_in_dim(x, mask, axis, keepdims=False)

        quads = PIECES // 2
        scalars = jnp.stack([mask_a, mask_b, z]).astype(jnp.int32)
        masks_v = scalars
        na = 2 * heads * E
        att = jnp.concatenate([f32(jnp.swapaxes(w_qkv, 1, 2)), f32(w_out)[None]])
        att = att.reshape(2, 2, heads, PIECES, E, D)
        att_piece = jnp.stack([pick(att[s], masks[s], 2).reshape(na, D) for s in (0, 1)])
        att_bufs = shards(att_piece)
        small = jnp.concatenate([f32(b_qv).reshape(-1), f32(b_up)])[None]
        for m in tp_bits:
            small = jnp.concatenate(
                [small, lax.ppermute(small, "tp", [(i, i ^ m) for i in range(T)])]
            )
        up_own = w_up.T.reshape(2, PIECES, FP, D)
        down_own = w_down.reshape(2, PIECES, FP, D)
        ffn_piece = jnp.stack(
            [
                jnp.concatenate([f32(pick(up_own[s], masks[s], 0)), f32(pick(down_own[s], masks[s], 0))])
                for s in (0, 1)
            ]
        )
        ffn_piece, *att_bufs = lax.optimization_barrier((ffn_piece, *att_bufs))
        ffn_bufs = shards(ffn_piece)
        shape = (2, quads, T - 1, 2, heads, E, D)
        both = swap_second(swap_first(att_bufs))
        other = swap(both, 0).reshape(shape)
        att_w = join_att(masks_v, att, both.reshape(shape), other)
        att_w = att_w.reshape(4 * T * width, D)
        wqkv_t = att_w[: 3 * T * width]
        wo = att_w[3 * T * width :]

        bq, bv, bup = bias_rows(
            scalars,
            small[:, :width].reshape(-1, E),
            small[:, width : 2 * width].reshape(-1, E),
            small[:, 2 * width :].reshape(-1, FP),
            T, heads, True,
        )
        bq, bv, bup = bq.reshape(-1), bv.reshape(-1), bup.reshape(-1)

        type_frac = f32(own_slice(type_ids, tokens))[:, None]
        segment = own_slice(segment_ids, nrows)
        table = f32(type_table)
        embedded = f32(own_slice(features, tokens)) + (table[0] + type_frac * (table[1] - table[0]))
        normal_in = bf16(embedded)
        C = T * width
        H = T * heads
        shape_four = (nrows, length, H, HEAD_DIM)
        ffn_both = swap_second(swap_first(ffn_bufs))
        queries = bf16(dot_t(normal_in, wqkv_t[:C]) + bq).reshape(shape_four)
        keys = bf16(dot_t(normal_in, wqkv_t[C : 2 * C])).reshape(shape_four)
        values = bf16(dot_t(normal_in, wqkv_t[2 * C :]) + bv).reshape(shape_four)
        scale = HEAD_DIM ** (-0.5)
        same = (segment[:, :, None] == segment[:, None, :])[:, None]
        scores = jnp.einsum("rqhd,rkhd->rhqk", queries, keys, preferred_element_type=jnp.float32)
        scores = jnp.where(same, scores * scale, NEG)
        highest = jnp.max(scores, axis=-1, keepdims=True)
        weights = jnp.exp(scores - highest)
        total = jnp.sum(weights, axis=-1, keepdims=True)
        weights = bf16(weights / total)
        attended = bf16(
            jnp.einsum("rhqk,rkhd->rqhd", weights, values, preferred_element_type=jnp.float32)
        ).reshape(tokens, C)
        ffn_other = swap(ffn_both, 0)
        shape = (2, quads, T - 1, 2, FP, D)
        up_t, down = (
            join_ffn(masks_v, own, ffn_both.reshape(shape), ffn_other.reshape(shape), i).reshape(-1, D)
            for i, own in enumerate((up_own, down_own))
        )
        attn_out = dot_n(attended, wo) + f32(b_out)
        normed_a, inverse_a = normalize(embedded + attn_out)
        gain_one = f32(gain_attn)
        normed_one = normed_a * gain_one + f32(shift_attn)
        ffn_in = bf16(normed_one)
        pre_act = dot_t(ffn_in, up_t) + bup
        cdf = 0.5 * (1.0 + lax.erf(pre_act * (0.5**0.5)))
        activated = bf16(pre_act * cdf)
        ffn_out = dot_n(activated, down) + f32(b_down)
        normed_b, inverse_b = normalize(normed_one + ffn_out)
        gain_two = f32(gain_ffn)
        out_own = normed_b * gain_two + f32(shift_ffn)
        gathered_out = lax.all_gather(out_own, "tp", axis=0, tiled=True)
        output = rounded(gathered_out)

        grad_out = f32(own_slice(cotangent, tokens))
        grad_shift_ffn = jnp.sum(grad_out, axis=0)
        grad_gain_ffn = jnp.sum(grad_out * normed_b, axis=0)
        grad_h2 = norm_back(grad_out * gain_two, normed_b, inverse_b)
        grad_b_down = jnp.sum(grad_h2, axis=0)
        grad_h2_low = bf16(grad_h2)
        half = T * shard_ff // 2
        six = (2, 2, 2, T, FP, D)
        gd_send = dot_a(activated[:, half:], grad_h2_low).reshape(six)
        gd_keep = dot_a(activated[:, :half], grad_h2_low).reshape(six)
        gd = halve_core(gd_keep, gd_send)
        gd = halve_second(halve_first(gd))
        grad_act = dot_t(grad_h2_low, down)
        pdf = jnp.exp(-0.5 * pre_act * pre_act) * (0.5 / jnp.pi) ** 0.5
        grad_pre = bf16(grad_act * (cdf + pre_act * pdf))
        grad_b_up = jnp.sum(f32(grad_pre), axis=0)
        gu_send = dot_a(grad_pre[:, half:], ffn_in).reshape(six)
        gu_keep = dot_a(grad_pre[:, :half], ffn_in).reshape(six)
        gu = halve_core(gu_keep, gu_send)
        gu = halve_second(halve_first(gu))
        gf = shard_sum([jnp.concatenate([u, d], axis=1) for u, d in zip(gu, gd)])
        grad_normed = grad_h2 + dot_n(grad_pre, up_t)
        grad_shift_attn = jnp.sum(grad_normed, axis=0)
        grad_gain_attn = jnp.sum(grad_normed * normed_a, axis=0)
        grad_h1 = norm_back(grad_normed * gain_one, normed_a, inverse_a)
        grad_b_out = jnp.sum(grad_h1, axis=0)
        grad_h1_low = bf16(grad_h1)
        grad_wo = dot_a(attended, grad_h1_low)
        grad_att = bf16(dot_t(grad_h1_low, wo)).reshape(shape_four)
        logsum = highest + jnp.log(total)
        probs = jnp.exp(scores - logsum)
        grad_weights = jnp.einsum(
            "rqhd,rkhd->rhqk", grad_att, values, preferred_element_type=jnp.float32
        )
        inner = jnp.sum(probs * grad_weights, axis=-1, keepdims=True)
        grad_scores = bf16(probs * (grad_weights - inner))
        grad_q = bf16(
            jnp.einsum("rhqk,rkhd->rqhd", grad_scores, keys, preferred_element_type=jnp.float32)
            * scale
        ).reshape(tokens, C)
        grad_k = bf16(
            jnp.einsum("rhqk,rqhd->rkhd", grad_scores, queries, preferred_element_type=jnp.float32)
            * scale
        ).reshape(tokens, C)
        grad_v = bf16(
            jnp.einsum("rhqk,rqhd->rkhd", bf16(probs), grad_att, preferred_element_type=jnp.float32)
        ).reshape(tokens, C)
        grad_proj = jnp.concatenate([grad_q, grad_k, grad_v], axis=1)
        grad_embedded = lax.optimization_barrier(grad_h1 + dot_n(grad_proj, wqkv_t))
        gathered = lax.all_gather(grad_embedded, "tp", axis=0, tiled=True)
        gq = dot_a(grad_proj, normal_in)
        ga = jnp.concatenate([gq, grad_wo]).reshape(2, 2, T, heads, 2, 2, 2, E, D)
        ga = ga.transpose(4, 0, 5, 6, 2, 1, 3, 7, 8).reshape(2, 2, 2, 2, T, na, D)
        ga = halve_second(halve_first(halve_core(ga[0], ga[1])))
        ga = shard_sum(ga)

        pieces = spread(gf)
        g_ffn = place(masks_v, *pieces)
        grad_w_up = g_ffn[:, :, :FP].reshape(shard_ff, D).T
        grad_w_down = g_ffn[:, :, FP:].reshape(shard_ff, D)
        g_att = place(masks_v, *spread(ga)).reshape(2, PIECES, 2, heads, E, D)
        g_att = g_att.transpose(0, 2, 3, 1, 4, 5).reshape(4, width, D)
        grad_qkv = jnp.swapaxes(g_att[:3], 1, 2)
        grad_w_out = g_att[3]

        gbq, gbv, gbup = bias_rows(
            scalars,
            jnp.sum(f32(grad_q), axis=0).reshape(-1, E),
            jnp.sum(f32(grad_v), axis=0).reshape(-1, E),
            grad_b_up.reshape(-1, FP),
            T, heads, False,
        )
        upper = jnp.sum(type_frac * grad_embedded, axis=0)
        lower = jnp.sum(grad_embedded, axis=0) - upper
        vec = pack(
            [
                lower, upper, grad_b_out, grad_gain_attn, grad_shift_attn, grad_b_down,
                grad_gain_ffn, grad_shift_ffn, gbq.reshape(-1), gbv.reshape(-1), gbup.reshape(-1),
            ],
            D,
        )
        vec = total_over(vec).reshape(-1)
        grad_features = rounded(gathered, vec, output, g_ffn)
        lines = vec[: 8 * D].reshape(8, D)
        gb = vec[8 * D : 8 * D + 2 * C].reshape(2, C)
        grad_bias_qv = lax.dynamic_slice_in_dim(gb, z * width, width, 1)
        grad_b_up = lax.dynamic_slice_in_dim(vec[8 * D + 2 * C :], z * shard_ff, shard_ff, 0)
        return (
            output, grad_features, lines[:2], grad_qkv, grad_bias_qv, grad_w_out, lines[2],
            lines[3], lines[4], grad_w_up, grad_b_up, grad_w_down, lines[5], lines[6], lines[7],
        )

    return per_device


def solution(mesh):
    in_specs = (
        P("rows", None), P("rows"), P("rows", None), P(), P(None, None, "tp"), P(None, "tp"),
        P("tp", None), P(), P(), P(), P(None, "tp"), P("tp"), P("tp", None), P(), P(), P(),
        P("rows", None),
    )
    out_specs = (
        P("rows", None), P("rows", None), P(), P(None, None, "tp"), P(None, "tp"), P("tp", None),
        P(), P(), P(), P(None, "tp"), P("tp"), P("tp", None), P(), P(), P(),
    )
    layer = make(mesh)

    return jax.shard_map(layer, mesh=mesh, in_specs=in_specs, out_specs=out_specs, check_vma=False)
```

profile of v0, /device:TPU:0, one launch (start us, length us, event | category | flops | bytes accessed | tf_op | source)
XLA Modules:
  0.0 704.7 jit_solution(15407691211149347291)
XLA Ops:
  24.7 10.8 %collective-permute-done.1 = f32[2,48,768]{2,1,0:T(8,128)} collective-permute-done((f32[2,48,768]{2,1,0:T(8,128)}, f32[2,48,768]{2,1,0:T(8,128)}, u32[]{:S(2)}, u32[]{:S(2)}) %collective-permute-start.1) | collective-permute-done | bytes 294944 | tf_op jit(solution)/shard_map/ppermute | solution.py:216
  37.5 5.8 collective-permute-start.10
  49.0 10.7 %collective-permute-done.10 = f32[2,96,768]{2,1,0:T(8,128)S(1)} collective-permute-done((f32[2,96,768]{2,1,0:T(8,128)S(1)}, f32[2,96,768]{2,1,0:T(8,128)S(1)}, u32[]{:S(2)}, u32[]{:S(2)}) %collective-permute-start.10) | collective-permute-done | bytes 589856 | tf_op jit(solution)/shard_map/ppermute | solution.py:216
  59.8 23.5 %collective-permute-done.11 = f32[2,96,768]{2,1,0:T(8,128)S(1)} collective-permute-done((f32[2,96,768]{2,1,0:T(8,128)S(1)}, f32[2,96,768]{2,1,0:T(8,128)S(1)}, u32[]{:S(2)}, u32[]{:S(2)}) %collective-permute-start.11) | collective-permute-done | bytes 589856 | tf_op jit(solution)/shard_map/ppermute | solution.py:216
  88.3 17.8 %collective-permute-done.13 = f32[3,96,768]{2,1,0:T(8,128)S(1)} collective-permute-done((f32[3,96,768]{2,1,0:T(8,128)S(1)}, f32[3,96,768]{2,1,0:T(8,128)S(1)}, u32[]{:S(2)}, u32[]{:S(2)}) %collective-permute-start.13) | collective-permute-done | bytes 884768 | tf_op jit(solution)/shard_map/ppermute | solution.py:213
  113.4 13.4 %collective-permute-done.4 = f32[2,3,48,768]{3,2,1,0:T(8,128)S(1)} collective-permute-done((f32[2,3,48,768]{3,2,1,0:T(8,128)S(1)}, f32[2,3,48,768]{3,2,1,0:T(8,128)S(1)}, u32[]{:S(2)}, u32[]{:S(2)}) %collective-permute-start.4) | collective-permute-done | bytes 884768 | tf_op jit(solution)/shard_map/ppermute | solution.py:213
  131.3 13.1 %collective-permute-start.8 = (f32[1,1152]{1,0:T(1,128)S(1)}, f32[1,1152]{1,0:T(1,128)}, u32[]{:S(2)}, u32[]{:S(2)}) collective-permute-start(f32[1,1152]{1,0:T(1,128)S(1)} %reshape.461), channel_id=1, source_target_pairs={{0,1},{1,0},{2,3},{3,2},{4,5},{5,4},{6,7},{7,6},{8,9},{9,8},{10,11... | collective-permute-start | bytes 13832 | tf_op jit(solution)/shard_map/ppermute | solution.py:293
  147.1 16.4 %collective-permute-done.14 = f32[2,3,96,768]{3,2,1,0:T(8,128)} collective-permute-done((f32[2,3,96,768]{3,2,1,0:T(8,128)}, f32[2,3,96,768]{3,2,1,0:T(8,128)}, u32[]{:S(2)}, u32[]{:S(2)}) %collective-permute-start.14) | collective-permute-done | bytes 1769504 | tf_op jit(solution)/shard_map/ppermute | solution.py:213
  163.5 4.4 fusion.102
  167.9 3.8 fusion.101
  180.2 12.2 %collective-permute-start.9 = (f32[2,1152]{1,0:T(2,128)S(1)}, f32[2,1152]{1,0:T(2,128)S(1)}, u32[]{:S(2)}, u32[]{:S(2)}) collective-permute-start(f32[2,1152]{1,0:T(2,128)S(1)} %pad_maximum_fusion.36), channel_id=1, source_target_pairs={{0,2},{1,3},{2,0},{3,1},{4,6},{5,7},{6,4},{7,5},{8,10},{9,11},{10,... | collective-permute-start | bytes 27656 | tf_op jit(solution)/shard_map/ppermute | solution.py:293
  203.9 4.0 pad_maximum_fusion.3.mine_ref
  211.9 7.1 %shard_map.280 = bf16[2,2,4,3,64,768]{5,4,3,2,1,0:T(8,128)(2,1)} custom-call(s32[3]{0:T(128)} %pad_add_fusion.masks_ref.scalars_ref, f32[2,2,3,8,8,768]{5,4,3,2,1,0:T(8,128)} %bitcast.291, f32[2,4,3,2,3,8,768]{6,5,4,3,2,1,0:T(8,128)} %pad_maximum_fusion.3.mine_ref, f32[2,4,3,2,3,8,768]{6,5,4,3,2,1,0:T(8,128)} %bitcast.33.other_ref), custom_call_target="tpu_custom_call" | custom-call | tf_op jit(solution)/shard_map/pallas_call | solution.py:151
  235.7 3.6 fusion.37
  242.4 5.8 shard_map.282
  248.2 6.3 shard_map.283
  254.6 5.5 multiply_convert_fusion.1
  266.5 5.3 convert_reduce_fusion
  271.8 3.6 multiply_reduce_fusion.1
  283.3 13.8 %multiply_reduce_fusion = (f32[12,512]{1,0:T(8,128)S(1)}, f32[12,512,512]{1,2,0:T(8,128)}) fusion(f32[12,512]{1,0:T(8,128)S(1)} %log_add_fusion, f32[12,512,512]{1,2,0:T(8,128)} %copy-done.2, pred[512,512]{0,1:T(8,128)(4,1)S(1)} %copy-done.13, bf16[512,12,64]{0,2,1:T(8,128)(2,1)} %bitcast.317, bf16[512,12,64]{0,2,1:T(8,128)(2,1)} %bitcast.316), kind=kOutput, calls=%fused_computation.1 | convolution fusion | flops 418375680 | bytes 27049984 | tf_op jit(solution)/shard_map/rqhd,rkhd->rhqk/dot_general | solution.py:397
  297.1 7.0 multiply_convert_fusion
  309.6 4.0 convert_reduce_fusion.2
  313.5 6.5 fusion.51
  320.0 8.1 %pad_maximum_fusion = f32[3072,768]{1,0:T(8,128)} fusion(f32[768,768]{1,0:T(8,128)} %fusion.68, f32[2304,768]{1,0:T(8,128)} %fusion.51), kind=kLoop, calls=%fused_computation.9 | loop fusion | flops 2359296 | bytes 18874368 | tf_op jit(solution)/shard_map/concatenate | solution.py:417
  328.1 4.8 fusion.111
  337.0 3.7 fusion.26
  341.0 3.5 fusion.22
  350.9 4.4 add.293
  361.2 3.6 fusion.24
  378.3 9.6 %collective-permute-done.42 = f32[2,4,48,768]{3,2,1,0:T(8,128)} collective-permute-done((f32[2,4,48,768]{3,2,1,0:T(8,128)}, f32[2,4,48,768]{3,2,1,0:T(8,128)}, u32[]{:S(2)}, u32[]{:S(2)}) %collective-permute-start.42) | collective-permute-done | bytes 1179680 | tf_op jit(solution)/shard_map/ppermute | solution.py:213
  392.4 20.6 %collective-permute-done.24 = f32[2,4,48,768]{3,2,1,0:T(8,128)S(1)} collective-permute-done((f32[2,4,48,768]{3,2,1,0:T(8,128)S(1)}, f32[2,4,48,768]{3,2,1,0:T(8,128)S(1)}, u32[]{:S(2)}, u32[]{:S(2)}) %collective-permute-start.24) | collective-permute-done | bytes 1179680 | tf_op jit(solution)/shard_map/ppermute | solution.py:213
  415.9 22.4 %collective-permute-done.27 = f32[2,4,48,768]{3,2,1,0:T(8,128)S(1)} collective-permute-done((f32[2,4,48,768]{3,2,1,0:T(8,128)S(1)}, f32[2,4,48,768]{3,2,1,0:T(8,128)S(1)}, u32[]{:S(2)}, u32[]{:S(2)}) %collective-permute-start.27) | collective-permute-done | bytes 1179680 | tf_op jit(solution)/shard_map/ppermute | solution.py:213
  441.9 21.7 %collective-permute-done.30 = f32[4,48,768]{2,1,0:T(8,128)S(1)} collective-permute-done((f32[4,48,768]{2,1,0:T(8,128)S(1)}, f32[4,48,768]{2,1,0:T(8,128)S(1)}, u32[]{:S(2)}, u32[]{:S(2)}) %collective-permute-start.30) | collective-permute-done | bytes 589856 | tf_op jit(solution)/shard_map/ppermute | solution.py:213
  464.6 10.9 %collective-permute-done.32 = f32[4,48,768]{2,1,0:T(8,128)S(1)} collective-permute-done((f32[4,48,768]{2,1,0:T(8,128)S(1)}, f32[4,48,768]{2,1,0:T(8,128)S(1)}, u32[]{:S(2)}, u32[]{:S(2)}) %collective-permute-start.32) | collective-permute-done | bytes 589856 | tf_op jit(solution)/shard_map/ppermute | solution.py:213
  485.4 23.4 %collective-permute-done.33 = f32[2,96,768]{2,1,0:T(8,128)S(1)} collective-permute-done((f32[2,96,768]{2,1,0:T(8,128)S(1)}, f32[2,96,768]{2,1,0:T(8,128)S(1)}, u32[]{:S(2)}, u32[]{:S(2)}) %collective-permute-start.33) | collective-permute-done | bytes 589856 | tf_op jit(solution)/shard_map/ppermute | solution.py:216
  508.7 12.2 %collective-permute-start.48 = (f32[2,48,768]{2,1,0:T(8,128)S(1)}, f32[2,48,768]{2,1,0:T(8,128)S(1)}, u32[]{:S(2)}, u32[]{:S(2)}) collective-permute-start(f32[2,48,768]{2,1,0:T(8,128)S(1)} %get-tuple-element.91), channel_id=1, source_target_pairs={{0,3},{1,0},{2,1},{3,2},{4,7},{5,4},{6,5},{7,6},{8,11},{9,8},{10,9... | collective-permute-start | bytes 884744 | tf_op jit(solution)/shard_map/ppermute | solution.py:216
  520.9 26.2 %collective-permute-done.34 = f32[2,96,768]{2,1,0:T(8,128)S(1)} collective-permute-done((f32[2,96,768]{2,1,0:T(8,128)S(1)}, f32[2,96,768]{2,1,0:T(8,128)S(1)}, u32[]{:S(2)}, u32[]{:S(2)}) %collective-permute-start.34) | collective-permute-done | bytes 589856 | tf_op jit(solution)/shard_map/ppermute | solution.py:216
  551.7 6.9 collective-permute-done.46
  558.6 24.2 %collective-permute-done.47 = f32[2,48,768]{2,1,0:T(8,128)S(1)} collective-permute-done((f32[2,48,768]{2,1,0:T(8,128)S(1)}, f32[2,48,768]{2,1,0:T(8,128)S(1)}, u32[]{:S(2)}, u32[]{:S(2)}) %collective-permute-start.47) | collective-permute-done | bytes 294944 | tf_op jit(solution)/shard_map/ppermute | solution.py:216
  587.3 15.5 %collective-permute-done.49 = f32[48,768]{1,0:T(8,128)S(1)} collective-permute-done((f32[48,768]{1,0:T(8,128)S(1)}, f32[48,768]{1,0:T(8,128)S(1)}, u32[]{:S(2)}, u32[]{:S(2)}) %collective-permute-start.49) | collective-permute-done | bytes 147488 | tf_op jit(solution)/shard_map/ppermute | solution.py:213
  605.6 5.3 collective-permute-done.50
  643.7 6.9 collective-permute-start.21
  654.3 4.3 collective-permute-done.22
  669.2 3.4 shard_map.289
  676.6 5.0 shard_map.284.refs_1_
  681.6 4.7 shard_map.287.refs_2_
  686.3 4.2 fusion.112
  692.4 5.0 shard_map.288
  (394 shorter events, 223.9 us)
Async XLA Ops:
  7.2 669.4 %all-gather.3.cloned.1.call-start = ((), (), s32[]{:S(2)}) async-start(), calls=%async_computation | async-start | bytes 7864320 | tf_op jit(solution)/shard_map/all_gather | solution.py:363
  13.3 22.1 %collective-permute-start.1 = (f32[2,48,768]{2,1,0:T(8,128)}, f32[2,48,768]{2,1,0:T(8,128)}, u32[]{:S(2)}, u32[]{:S(2)}) collective-permute-start(f32[2,48,768]{2,1,0:T(8,128)} %pad_maximum_fusion.31), channel_id=1, source_target_pairs={{0,2},{1,3},{2,0},{3,1},{4,6},{5,7},{6,4},{7,5},{8,10},{9,11},{10,... | collective-permute-start | bytes 884744 | tf_op jit(solution)/shard_map/ppermute | solution.py:216
  15.9 20.5 %collective-permute-start.2 = (f32[2,48,768]{2,1,0:T(8,128)}, f32[2,48,768]{2,1,0:T(8,128)}, u32[]{:S(2)}, u32[]{:S(2)}) collective-permute-start(f32[2,48,768]{2,1,0:T(8,128)} %pad_maximum_fusion.31), channel_id=1, source_target_pairs={{0,3},{1,0},{2,1},{3,2},{4,7},{5,4},{6,5},{7,6},{8,11},{9,8},{10,9... | collective-permute-start | bytes 884744 | tf_op jit(solution)/shard_map/ppermute | solution.py:216
  37.5 22.2 %collective-permute-start.10 = (f32[2,96,768]{2,1,0:T(8,128)S(1)}, f32[2,96,768]{2,1,0:T(8,128)S(1)}, u32[]{:S(2)}, u32[]{:S(2)}) collective-permute-start(f32[2,96,768]{2,1,0:T(8,128)S(1)} %maximum_convert_fusion), channel_id=1, source_target_pairs={{0,1},{1,2},{2,3},{3,0},{4,5},{5,6},{6,7},{7,4},{8,9},{9,10},{10,1... | collective-permute-start | bytes 1769480 | tf_op jit(solution)/shard_map/ppermute | solution.py:216
  43.4 39.9 %collective-permute-start.11 = (f32[2,96,768]{2,1,0:T(8,128)S(1)}, f32[2,96,768]{2,1,0:T(8,128)S(1)}, u32[]{:S(2)}, u32[]{:S(2)}) collective-permute-start(f32[2,96,768]{2,1,0:T(8,128)S(1)} %maximum_convert_fusion), channel_id=1, source_target_pairs={{0,2},{1,3},{2,0},{3,1},{4,6},{5,7},{6,4},{7,5},{8,10},{9,11},{10,... | collective-permute-start | bytes 1769480 | tf_op jit(solution)/shard_map/ppermute | solution.py:216
  46.0 37.4 %collective-permute-start.12 = (f32[2,96,768]{2,1,0:T(8,128)S(1)}, f32[2,96,768]{2,1,0:T(8,128)S(1)}, u32[]{:S(2)}, u32[]{:S(2)}) collective-permute-start(f32[2,96,768]{2,1,0:T(8,128)S(1)} %maximum_convert_fusion), channel_id=1, source_target_pairs={{0,3},{1,0},{2,1},{3,2},{4,7},{5,4},{6,5},{7,6},{8,11},{9,8},{10,9... | collective-permute-start | bytes 1769480 | tf_op jit(solution)/shard_map/ppermute | solution.py:216
  46.0 40.9 %collective-permute-start.3 = (f32[3,48,768]{2,1,0:T(8,128)S(1)}, f32[3,48,768]{2,1,0:T(8,128)S(1)}, u32[]{:S(2)}, u32[]{:S(2)}) collective-permute-start(f32[3,48,768]{2,1,0:T(8,128)S(1)} %get-tuple-element.24), channel_id=1, source_target_pairs={{0,8},{4,12},{8,0},{12,4},{16,24},{20,28},{24,16},{28,20},{1,9},{5... | collective-permute-start | bytes 1327112 | tf_op jit(solution)/shard_map/ppermute | solution.py:213
  47.5 40.1 %collective-permute-start.5 = (f32[3,48,768]{2,1,0:T(8,128)S(1)}, f32[3,48,768]{2,1,0:T(8,128)S(1)}, u32[]{:S(2)}, u32[]{:S(2)}) collective-permute-start(f32[3,48,768]{2,1,0:T(8,128)S(1)} %get-tuple-element.25), channel_id=1, source_target_pairs={{0,16},{4,20},{8,24},{12,28},{16,0},{20,4},{24,8},{28,12},{1,17},{... | collective-permute-start | bytes 1327112 | tf_op jit(solution)/shard_map/ppermute | solution.py:213
  83.6 22.6 %collective-permute-start.13 = (f32[3,96,768]{2,1,0:T(8,128)S(1)}, f32[3,96,768]{2,1,0:T(8,128)S(1)}, u32[]{:S(2)}, u32[]{:S(2)}) collective-permute-start(f32[3,96,768]{2,1,0:T(8,128)S(1)} %get-tuple-element.97), channel_id=1, source_target_pairs={{0,8},{4,12},{8,0},{12,4},{16,24},{20,28},{24,16},{28,20},{1,9},{5... | collective-permute-start | bytes 2654216 | tf_op jit(solution)/shard_map/ppermute | solution.py:213
  85.3 24.5 %collective-permute-start.15 = (f32[3,96,768]{2,1,0:T(8,128)S(1)}, f32[3,96,768]{2,1,0:T(8,128)S(1)}, u32[]{:S(2)}, u32[]{:S(2)}) collective-permute-start(f32[3,96,768]{2,1,0:T(8,128)S(1)} %get-tuple-element.99), channel_id=1, source_target_pairs={{0,16},{4,20},{8,24},{12,28},{16,0},{20,4},{24,8},{28,12},{1,17},{... | collective-permute-start | bytes 2654216 | tf_op jit(solution)/shard_map/ppermute | solution.py:213
  87.0 39.8 %collective-permute-start.4 = (f32[2,3,48,768]{3,2,1,0:T(8,128)S(1)}, f32[2,3,48,768]{3,2,1,0:T(8,128)S(1)}, u32[]{:S(2)}, u32[]{:S(2)}) collective-permute-start(f32[2,3,48,768]{3,2,1,0:T(8,128)S(1)} %get-tuple-element.101), channel_id=1, source_target_pairs={{0,16},{4,20},{8,24},{12,28},{16,0},{20,4},{24,8},{28,12},{1,17},{... | collective-permute-start | bytes 2654216 | tf_op jit(solution)/shard_map/ppermute | solution.py:213
  87.7 39.3 %collective-permute-start.6 = (f32[2,3,48,768]{3,2,1,0:T(8,128)S(1)}, f32[2,3,48,768]{3,2,1,0:T(8,128)S(1)}, u32[]{:S(2)}, u32[]{:S(2)}) collective-permute-start(f32[2,3,48,768]{3,2,1,0:T(8,128)S(1)} %get-tuple-element.103), channel_id=1, source_target_pairs={{0,8},{4,12},{8,0},{12,4},{16,24},{20,28},{24,16},{28,20},{1,9},{5... | collective-permute-start | bytes 2654216 | tf_op jit(solution)/shard_map/ppermute | solution.py:213
  108.3 55.3 %collective-permute-start.14 = (f32[2,3,96,768]{3,2,1,0:T(8,128)}, f32[2,3,96,768]{3,2,1,0:T(8,128)}, u32[]{:S(2)}, u32[]{:S(2)}) collective-permute-start(f32[2,3,96,768]{3,2,1,0:T(8,128)} %get-tuple-element.79), channel_id=1, source_target_pairs={{0,16},{4,20},{8,24},{12,28},{16,0},{20,4},{24,8},{28,12},{1,17},{... | collective-permute-start | bytes 5308424 | tf_op jit(solution)/shard_map/ppermute | solution.py:213
  111.9 56.0 %collective-permute-start.16 = (f32[2,3,96,768]{3,2,1,0:T(8,128)}, f32[2,3,96,768]{3,2,1,0:T(8,128)}, u32[]{:S(2)}, u32[]{:S(2)}) collective-permute-start(f32[2,3,96,768]{3,2,1,0:T(8,128)} %get-tuple-element.81), channel_id=1, source_target_pairs={{0,8},{4,12},{8,0},{12,4},{16,24},{20,28},{24,16},{28,20},{1,9},{5... | collective-permute-start | bytes 5308424 | tf_op jit(solution)/shard_map/ppermute | solution.py:213
  130.5 81.3 %collective-permute-start.7 = (f32[2,2,2,3,48,768]{5,4,3,2,1,0:T(8,128)}, f32[2,2,2,3,48,768]{5,4,3,2,1,0:T(8,128)}, u32[]{:S(2)}, u32[]{:S(2)}) collective-permute-start(f32[2,2,2,3,48,768]{5,4,3,2,1,0:T(8,128)} %pad_maximum_fusion.4), channel_id=1, source_target_pairs={{0,4},{4,0},{8,12},{12,8},{16,20},{20,16},{24,28},{28,24},{1,5},{5... | collective-permute-start | bytes 10616840 | tf_op jit(solution)/shard_map/ppermute | solution.py:213
  131.3 48.2 %collective-permute-start.8 = (f32[1,1152]{1,0:T(1,128)S(1)}, f32[1,1152]{1,0:T(1,128)}, u32[]{:S(2)}, u32[]{:S(2)}) collective-permute-start(f32[1,1152]{1,0:T(1,128)S(1)} %reshape.461), channel_id=1, source_target_pairs={{0,1},{1,0},{2,3},{3,2},{4,5},{5,4},{6,7},{7,6},{8,9},{9,8},{10,11... | collective-permute-start | bytes 13832 | tf_op jit(solution)/shard_map/ppermute | solution.py:293
  175.1 67.3 %collective-permute-start.17 = (f32[2,2,2,3,96,768]{5,4,3,2,1,0:T(8,128)}, f32[2,2,2,3,96,768]{5,4,3,2,1,0:T(8,128)}, u32[]{:S(2)}, u32[]{:S(2)}) collective-permute-start(f32[2,2,2,3,96,768]{5,4,3,2,1,0:T(8,128)} %pad_maximum_fusion.2), channel_id=1, source_target_pairs={{0,4},{4,0},{8,12},{12,8},{16,20},{20,16},{24,28},{28,24},{1,5},{5... | collective-permute-start | bytes 21233672 | tf_op jit(solution)/shard_map/ppermute | solution.py:213
  180.2 15.3 %collective-permute-start.9 = (f32[2,1152]{1,0:T(2,128)S(1)}, f32[2,1152]{1,0:T(2,128)S(1)}, u32[]{:S(2)}, u32[]{:S(2)}) collective-permute-start(f32[2,1152]{1,0:T(2,128)S(1)} %pad_maximum_fusion.36), channel_id=1, source_target_pairs={{0,2},{1,3},{2,0},{3,1},{4,6},{5,7},{6,4},{7,5},{8,10},{9,11},{10,... | collective-permute-start | bytes 27656 | tf_op jit(solution)/shard_map/ppermute | solution.py:293
  283.0 409.4 %all-gather.5.cloned.1.call-start = ((), (), s32[]{:S(2)}) async-start(), calls=%async_computation.1 | async-start | bytes 7864320 | tf_op jit(solution)/shard_map/all_gather | solution.py:415
  336.0 14.9 %collective-permute-start.41 = (f32[2,2,2,4,48,768]{5,4,3,2,1,0:T(8,128)}, f32[2,2,2,4,48,768]{5,4,3,2,1,0:T(8,128)}, u32[]{:S(2)}, u32[]{:S(2)}) collective-permute-start(f32[2,2,2,4,48,768]{5,4,3,2,1,0:T(8,128)} %bitcast.114), channel_id=1, source_target_pairs={{0,4},{4,0},{8,12},{12,8},{16,20},{20,16},{24,28},{28,24},{1,5},{5... | collective-permute-start | bytes 14155784 | tf_op jit(solution)/shard_map/ppermute | solution.py:213
  340.8 27.3 %collective-permute-start.23 = (f32[2,2,2,4,48,768]{5,4,3,2,1,0:T(8,128)}, f32[2,2,2,4,48,768]{5,4,3,2,1,0:T(8,128)}, u32[]{:S(2)}, u32[]{:S(2)}) collective-permute-start(f32[2,2,2,4,48,768]{5,4,3,2,1,0:T(8,128)} %bitcast.72), channel_id=1, source_target_pairs={{0,4},{4,0},{8,12},{12,8},{16,20},{20,16},{24,28},{28,24},{1,5},{5... | collective-permute-start | bytes 14155784 | tf_op jit(solution)/shard_map/ppermute | solution.py:213
  344.5 28.7 %collective-permute-start.26 = (f32[2,2,2,4,48,768]{5,4,3,2,1,0:T(8,128)}, f32[2,2,2,4,48,768]{5,4,3,2,1,0:T(8,128)}, u32[]{:S(2)}, u32[]{:S(2)}) collective-permute-start(f32[2,2,2,4,48,768]{5,4,3,2,1,0:T(8,128)} %bitcast.78), channel_id=1, source_target_pairs={{0,4},{4,0},{8,12},{12,8},{16,20},{20,16},{24,28},{28,24},{1,5},{5... | collective-permute-start | bytes 14155784 | tf_op jit(solution)/shard_map/ppermute | solution.py:213
  358.7 29.2 %collective-permute-start.42 = (f32[2,4,48,768]{3,2,1,0:T(8,128)}, f32[2,4,48,768]{3,2,1,0:T(8,128)}, u32[]{:S(2)}, u32[]{:S(2)}) collective-permute-start(f32[2,4,48,768]{3,2,1,0:T(8,128)} %get-tuple-element.62), channel_id=1, source_target_pairs={{0,16},{4,20},{8,24},{12,28},{16,0},{20,4},{24,8},{28,12},{1,17},{... | collective-permute-start | bytes 3538952 | tf_op jit(solution)/shard_map/ppermute | solution.py:213
  360.3 29.2 %collective-permute-start.44 = (f32[2,4,48,768]{3,2,1,0:T(8,128)}, f32[2,4,48,768]{3,2,1,0:T(8,128)}, u32[]{:S(2)}, u32[]{:S(2)}) collective-permute-start(f32[2,4,48,768]{3,2,1,0:T(8,128)} %get-tuple-element.61), channel_id=1, source_target_pairs={{0,8},{4,12},{8,0},{12,4},{16,24},{20,28},{24,16},{28,20},{1,9},{5... | collective-permute-start | bytes 3538952 | tf_op jit(solution)/shard_map/ppermute | solution.py:213
  371.6 41.5 %collective-permute-start.24 = (f32[2,4,48,768]{3,2,1,0:T(8,128)S(1)}, f32[2,4,48,768]{3,2,1,0:T(8,128)S(1)}, u32[]{:S(2)}, u32[]{:S(2)}) collective-permute-start(f32[2,4,48,768]{3,2,1,0:T(8,128)S(1)} %get-tuple-element.66), channel_id=1, source_target_pairs={{0,16},{4,20},{8,24},{12,28},{16,0},{20,4},{24,8},{28,12},{1,17},{... | collective-permute-start | bytes 3538952 | tf_op jit(solution)/shard_map/ppermute | solution.py:213
  372.2 42.5 %collective-permute-start.29 = (f32[2,4,48,768]{3,2,1,0:T(8,128)S(1)}, f32[2,4,48,768]{3,2,1,0:T(8,128)S(1)}, u32[]{:S(2)}, u32[]{:S(2)}) collective-permute-start(f32[2,4,48,768]{3,2,1,0:T(8,128)S(1)} %get-tuple-element.65), channel_id=1, source_target_pairs={{0,8},{4,12},{8,0},{12,4},{16,24},{20,28},{24,16},{28,20},{1,9},{5... | collective-permute-start | bytes 3538952 | tf_op jit(solution)/shard_map/ppermute | solution.py:213
  376.6 61.7 %collective-permute-start.27 = (f32[2,4,48,768]{3,2,1,0:T(8,128)S(1)}, f32[2,4,48,768]{3,2,1,0:T(8,128)S(1)}, u32[]{:S(2)}, u32[]{:S(2)}) collective-permute-start(f32[2,4,48,768]{3,2,1,0:T(8,128)S(1)} %get-tuple-element.70), channel_id=1, source_target_pairs={{0,16},{4,20},{8,24},{12,28},{16,0},{20,4},{24,8},{28,12},{1,17},{... | collective-permute-start | bytes 3538952 | tf_op jit(solution)/shard_map/ppermute | solution.py:213
  387.9 52.1 %collective-permute-start.31 = (f32[2,4,48,768]{3,2,1,0:T(8,128)S(1)}, f32[2,4,48,768]{3,2,1,0:T(8,128)S(1)}, u32[]{:S(2)}, u32[]{:S(2)}) collective-permute-start(f32[2,4,48,768]{3,2,1,0:T(8,128)S(1)} %get-tuple-element.69), channel_id=1, source_target_pairs={{0,8},{4,12},{8,0},{12,4},{16,24},{20,28},{24,16},{28,20},{1,9},{5... | collective-permute-start | bytes 3538952 | tf_op jit(solution)/shard_map/ppermute | solution.py:213
  391.5 91.1 %collective-permute-start.45 = (f32[4,48,768]{2,1,0:T(8,128)S(1)}, f32[4,48,768]{2,1,0:T(8,128)S(1)}, u32[]{:S(2)}, u32[]{:S(2)}) collective-permute-start(f32[4,48,768]{2,1,0:T(8,128)S(1)} %slice_bitcast_fusion.14), channel_id=1, source_target_pairs={{0,16},{4,20},{8,24},{12,28},{16,0},{20,4},{24,8},{28,12},{1,17},{... | collective-permute-start | bytes 1769480 | tf_op jit(solution)/shard_map/ppermute | solution.py:213
  413.1 69.6 %collective-permute-start.43 = (f32[4,48,768]{2,1,0:T(8,128)S(1)}, f32[4,48,768]{2,1,0:T(8,128)S(1)}, u32[]{:S(2)}, u32[]{:S(2)}) collective-permute-start(f32[4,48,768]{2,1,0:T(8,128)S(1)} %slice_bitcast_fusion.16), channel_id=1, source_target_pairs={{0,8},{4,12},{8,0},{12,4},{16,24},{20,28},{24,16},{28,20},{1,9},{5... | collective-permute-start | bytes 1769480 | tf_op jit(solution)/shard_map/ppermute | solution.py:213
  415.0 48.6 %collective-permute-start.30 = (f32[4,48,768]{2,1,0:T(8,128)S(1)}, f32[4,48,768]{2,1,0:T(8,128)S(1)}, u32[]{:S(2)}, u32[]{:S(2)}) collective-permute-start(f32[4,48,768]{2,1,0:T(8,128)S(1)} %slice_bitcast_fusion.20), channel_id=1, source_target_pairs={{0,16},{4,20},{8,24},{12,28},{16,0},{20,4},{24,8},{28,12},{1,17},{... | collective-permute-start | bytes 1769480 | tf_op jit(solution)/shard_map/ppermute | solution.py:213
  440.3 35.2 %collective-permute-start.32 = (f32[4,48,768]{2,1,0:T(8,128)S(1)}, f32[4,48,768]{2,1,0:T(8,128)S(1)}, u32[]{:S(2)}, u32[]{:S(2)}) collective-permute-start(f32[4,48,768]{2,1,0:T(8,128)S(1)} %slice_bitcast_fusion.18), channel_id=1, source_target_pairs={{0,16},{4,20},{8,24},{12,28},{16,0},{20,4},{24,8},{28,12},{1,17},{... | collective-permute-start | bytes 1769480 | tf_op jit(solution)/shard_map/ppermute | solution.py:213
  440.9 34.8 %collective-permute-start.25 = (f32[4,48,768]{2,1,0:T(8,128)S(1)}, f32[4,48,768]{2,1,0:T(8,128)S(1)}, u32[]{:S(2)}, u32[]{:S(2)}) collective-permute-start(f32[4,48,768]{2,1,0:T(8,128)S(1)} %slice_bitcast_fusion.24), channel_id=1, source_target_pairs={{0,8},{4,12},{8,0},{12,4},{16,24},{20,28},{24,16},{28,20},{1,9},{5... | collective-permute-start | bytes 1769480 | tf_op jit(solution)/shard_map/ppermute | solution.py:213
  463.6 14.0 %collective-permute-start.28 = (f32[4,48,768]{2,1,0:T(8,128)S(1)}, f32[4,48,768]{2,1,0:T(8,128)S(1)}, u32[]{:S(2)}, u32[]{:S(2)}) collective-permute-start(f32[4,48,768]{2,1,0:T(8,128)S(1)} %slice_bitcast_fusion.22), channel_id=1, source_target_pairs={{0,8},{4,12},{8,0},{12,4},{16,24},{20,28},{24,16},{28,20},{1,9},{5... | collective-permute-start | bytes 1769480 | tf_op jit(solution)/shard_map/ppermute | solution.py:213
  478.0 30.7 %collective-permute-start.33 = (f32[2,96,768]{2,1,0:T(8,128)S(1)}, f32[2,96,768]{2,1,0:T(8,128)S(1)}, u32[]{:S(2)}, u32[]{:S(2)}) collective-permute-start(f32[2,96,768]{2,1,0:T(8,128)S(1)} %get-tuple-element.76), channel_id=1, source_target_pairs={{0,1},{1,2},{2,3},{3,0},{4,5},{5,6},{6,7},{7,4},{8,9},{9,10},{10,1... | collective-permute-start | bytes 1769480 | tf_op jit(solution)/shard_map/ppermute | solution.py:216
  480.1 67.0 %collective-permute-start.34 = (f32[2,96,768]{2,1,0:T(8,128)S(1)}, f32[2,96,768]{2,1,0:T(8,128)S(1)}, u32[]{:S(2)}, u32[]{:S(2)}) collective-permute-start(f32[2,96,768]{2,1,0:T(8,128)S(1)} %get-tuple-element.75), channel_id=1, source_target_pairs={{0,2},{1,3},{2,0},{3,1},{4,6},{5,7},{6,4},{7,5},{8,10},{9,11},{10,... | collective-permute-start | bytes 1769480 | tf_op jit(solution)/shard_map/ppermute | solution.py:216
  482.0 66.2 %collective-permute-start.35 = (f32[2,96,768]{2,1,0:T(8,128)S(1)}, f32[2,96,768]{2,1,0:T(8,128)S(1)}, u32[]{:S(2)}, u32[]{:S(2)}) collective-permute-start(f32[2,96,768]{2,1,0:T(8,128)S(1)} %get-tuple-element.77), channel_id=1, source_target_pairs={{0,3},{1,0},{2,1},{3,2},{4,7},{5,4},{6,5},{7,6},{8,11},{9,8},{10,9... | collective-permute-start | bytes 1769480 | tf_op jit(solution)/shard_map/ppermute | solution.py:216
  482.8 75.8 %collective-permute-start.46 = (f32[2,48,768]{2,1,0:T(8,128)S(1)}, f32[2,48,768]{2,1,0:T(8,128)S(1)}, u32[]{:S(2)}, u32[]{:S(2)}) collective-permute-start(f32[2,48,768]{2,1,0:T(8,128)S(1)} %get-tuple-element.90), channel_id=1, source_target_pairs={{0,1},{1,2},{2,3},{3,0},{4,5},{5,6},{6,7},{7,4},{8,9},{9,10},{10,1... | collective-permute-start | bytes 884744 | tf_op jit(solution)/shard_map/ppermute | solution.py:216
  484.3 98.4 %collective-permute-start.47 = (f32[2,48,768]{2,1,0:T(8,128)S(1)}, f32[2,48,768]{2,1,0:T(8,128)S(1)}, u32[]{:S(2)}, u32[]{:S(2)}) collective-permute-start(f32[2,48,768]{2,1,0:T(8,128)S(1)} %get-tuple-element.89), channel_id=1, source_target_pairs={{0,2},{1,3},{2,0},{3,1},{4,6},{5,7},{6,4},{7,5},{8,10},{9,11},{10,... | collective-permute-start | bytes 884744 | tf_op jit(solution)/shard_map/ppermute | solution.py:216
  508.7 74.0 %collective-permute-start.48 = (f32[2,48,768]{2,1,0:T(8,128)S(1)}, f32[2,48,768]{2,1,0:T(8,128)S(1)}, u32[]{:S(2)}, u32[]{:S(2)}) collective-permute-start(f32[2,48,768]{2,1,0:T(8,128)S(1)} %get-tuple-element.91), channel_id=1, source_target_pairs={{0,3},{1,0},{2,1},{3,2},{4,7},{5,4},{6,5},{7,6},{8,11},{9,8},{10,9... | collective-permute-start | bytes 884744 | tf_op jit(solution)/shard_map/ppermute | solution.py:216
  548.5 34.3 %collective-permute-start.36 = (f32[96,768]{1,0:T(8,128)S(1)}, f32[96,768]{1,0:T(8,128)S(1)}, u32[]{:S(2)}, u32[]{:S(2)}) collective-permute-start(f32[96,768]{1,0:T(8,128)S(1)} %get-tuple-element.107), channel_id=1, source_target_pairs={{0,8},{4,12},{8,0},{12,4},{16,24},{20,28},{24,16},{28,20},{1,9},{5... | collective-permute-start | bytes 884744 | tf_op jit(solution)/shard_map/ppermute | solution.py:213
  550.2 34.3 %collective-permute-start.38 = (f32[96,768]{1,0:T(8,128)S(1)}, f32[96,768]{1,0:T(8,128)S(1)}, u32[]{:S(2)}, u32[]{:S(2)}) collective-permute-start(f32[96,768]{1,0:T(8,128)S(1)} %get-tuple-element.108), channel_id=1, source_target_pairs={{0,16},{4,20},{8,24},{12,28},{16,0},{20,4},{24,8},{28,12},{1,17},{... | collective-permute-start | bytes 884744 | tf_op jit(solution)/shard_map/ppermute | solution.py:213
  582.9 20.6 %collective-permute-start.37 = (f32[2,96,768]{2,1,0:T(8,128)S(1)}, f32[2,96,768]{2,1,0:T(8,128)S(1)}, u32[]{:S(2)}, u32[]{:S(2)}) collective-permute-start(f32[2,96,768]{2,1,0:T(8,128)S(1)} %get-tuple-element.105), channel_id=1, source_target_pairs={{0,16},{4,20},{8,24},{12,28},{16,0},{20,4},{24,8},{28,12},{1,17},{... | collective-permute-start | bytes 1769480 | tf_op jit(solution)/shard_map/ppermute | solution.py:213
  584.6 19.1 %collective-permute-start.39 = (f32[2,96,768]{2,1,0:T(8,128)S(1)}, f32[2,96,768]{2,1,0:T(8,128)S(1)}, u32[]{:S(2)}, u32[]{:S(2)}) collective-permute-start(f32[2,96,768]{2,1,0:T(8,128)S(1)} %get-tuple-element.111), channel_id=1, source_target_pairs={{0,8},{4,12},{8,0},{12,4},{16,24},{20,28},{24,16},{28,20},{1,9},{5... | collective-permute-start | bytes 1769480 | tf_op jit(solution)/shard_map/ppermute | solution.py:213
  586.2 16.7 %collective-permute-start.49 = (f32[48,768]{1,0:T(8,128)S(1)}, f32[48,768]{1,0:T(8,128)S(1)}, u32[]{:S(2)}, u32[]{:S(2)}) collective-permute-start(f32[48,768]{1,0:T(8,128)S(1)} %get-tuple-element.121), channel_id=1, source_target_pairs={{0,8},{4,12},{8,0},{12,4},{16,24},{20,28},{24,16},{28,20},{1,9},{5... | collective-permute-start | bytes 442376 | tf_op jit(solution)/shard_map/ppermute | solution.py:213
  586.8 17.2 %collective-permute-start.51 = (f32[48,768]{1,0:T(8,128)S(1)}, f32[48,768]{1,0:T(8,128)S(1)}, u32[]{:S(2)}, u32[]{:S(2)}) collective-permute-start(f32[48,768]{1,0:T(8,128)S(1)} %get-tuple-element.122), channel_id=1, source_target_pairs={{0,16},{4,20},{8,24},{12,28},{16,0},{20,4},{24,8},{28,12},{1,17},{... | collective-permute-start | bytes 442376 | tf_op jit(solution)/shard_map/ppermute | solution.py:213
  603.9 77.7 %collective-permute-start.40 = (f32[2,4,96,768]{3,2,1,0:T(8,128)S(1)}, f32[2,4,96,768]{3,2,1,0:T(8,128)}, u32[]{:S(2)}, u32[]{:S(2)}) collective-permute-start(f32[2,4,96,768]{3,2,1,0:T(8,128)S(1)} %pad_maximum_fusion.9.mine_ref), channel_id=1, source_target_pairs={{0,4},{4,0},{8,12},{12,8},{16,20},{20,16},{24,28},{28,24},{1,5},{5... | collective-permute-start | bytes 7077896 | tf_op jit(solution)/shard_map/ppermute | solution.py:213
  613.7 55.5 %collective-permute-start.53 = (f32[2,4,48,768]{3,2,1,0:T(8,128)S(1)}, f32[2,4,48,768]{3,2,1,0:T(8,128)}, u32[]{:S(2)}, u32[]{:S(2)}) collective-permute-start(f32[2,4,48,768]{3,2,1,0:T(8,128)S(1)} %pad_maximum_fusion.16.mine_ref), channel_id=1, source_target_pairs={{0,4},{4,0},{8,12},{12,8},{16,20},{20,16},{24,28},{28,24},{1,5},{5... | collective-permute-start | bytes 3538952 | tf_op jit(solution)/shard_map/ppermute | solution.py:213
  (76 other events, 888.9 us)
Sparse Core Ops, SparseCore 0:
  283.1 115.4 all-gather.2
  400.2 167.9 all-gather.4
where the time goes:
time: 713 us; the launch traced here: 705 us
  waiting for transfers between devices  304 us (43%)
  starting transfers between devices  104 us (15%)
  other arithmetic  84.2 us (12%)
  matrix products  83.6 us (12%)
  local copies, waits for them, and re-layouts  71.3 us (10%)
  Pallas kernels  41.9 us (6%)
  between operations  15.8 us (2%)
    ppermute x38, waiting for transfers between devices, swap(): return lax.ppermute(x, 'rows', [(i, i ^ 1 << bit) for i in range(rows)])  168 us
    ppermute x12, waiting for transfers between devices, shift(): return lax.ppermute(x, 'tp', [(i, (i + k) % T) for i in range(T)])  130 us
    ppermute x38, starting transfers between devices, swap(): return lax.ppermute(x, 'rows', [(i, i ^ 1 << bit) for i in range(rows)])  36 us
    ppermute x12, starting transfers between devices, shift(): return lax.ppermute(x, 'tp', [(i, (i + k) % T) for i in range(T)])  34.7 us
    ppermute x2, starting transfers between devices, per_device(): lax.ppermute(small, 'tp', [(i, i ^ m) for i in range(T)])  25.3 us
    dot_general x6, matrix products, dot_a(): lax.dot_general(a, b, (((0,), (0,)), ((), ())), preferred_element_type=jn...  22.8 us
    another operation x10, other arithmetic, swap_second(): jnp.stack([jnp.stack([b, swap(b, bit)]) for b, bit in zip(bufs, (2, 1))])  22.8 us
    dot_general x6, matrix products, dot_t(): lax.dot_general(a, b, (((1,), (1,)), ((), ())), preferred_element_type=jn...  21.8 us
  transfers between devices with their start and end apart: 56, of which 29 were waited for; matrix products, arithmetic and copies ran while one was open for 28% of the time, Pallas kernels for 4%

commit v1 on v0

--- a/solution.py
+++ b/solution.py
@@ -50,6 +50,24 @@
         out_specs=pl.BlockSpec((block, d), lambda i: (i, 0)),
         out_shape=jax.ShapeDtypeStruct((n, d), jnp.bfloat16),
     )(x, *deps)
+
+
+def sum_kernel(a_ref, ra_ref, b_ref, rb_ref, o_ref):
+    o_ref[:, 0] = a_ref[0] + ra_ref[...]
+    o_ref[:, 1] = b_ref[0] + rb_ref[...]
+
+
+def sum_sets(accs, received):
+    _, t, n, d = accs[0].shape
+    kept = pl.BlockSpec((1, t, n, d), lambda i: (0, 0, 0, 0))
+    other = pl.BlockSpec((t, n, d), lambda i: (0, 0, 0))
+    return pl.pallas_call(
+        sum_kernel,
+        grid=(1,),
+        in_specs=[kept, other, kept, other],
+        out_specs=pl.BlockSpec((t, 2, n, d), lambda i: (0, 0, 0, 0)),
+        out_shape=jax.ShapeDtypeStruct((t, 2, n, d), jnp.float32),
+    )(accs[0], received[0], accs[1], received[1])
 
 
 def pack_kernel(*refs):
@@ -111,9 +129,9 @@
     o_ref[1, 0, :, 1:] = other_ref[0, :, :, 0].astype(jnp.bfloat16)
 
 
-def join_ffn(masks, own, mine, other, which):
+def join_ffn(masks, own, mine, other):
     _, quads, others, _, n, d = mine.shape
-    spec = pl.BlockSpec((1, quads, others, 1, n, d), lambda s, m: (s, 0, 0, which, 0, 0))
+    spec = pl.BlockSpec((1, quads, others, 1, n, d), lambda s, m: (s, 0, 0, 0, 0, 0))
     return pl.pallas_call(
         join_ffn_kernel,
         grid_spec=pltpu.PrefetchScalarGridSpec(
@@ -226,10 +244,9 @@
         return jnp.stack([jnp.stack([b, swap(b, bit)]) for b, bit in zip(bufs, (2, 1))])
 
     def total_over(x):
+        x = x + sum(shift(x, k) for k in range(1, T))
         for bit in range(row_bits):
             x = x + swap(x, bit)
-        for m in tp_bits:
-            x = x + lax.ppermute(x, "tp", [(i, i ^ m) for i in range(T)])
         return x
 
     def halve_core(keep, send):
@@ -241,9 +258,11 @@
     def halve_second(accs):
         return [acc[0] + swap(acc[1], bit) for acc, bit in zip(accs, (1, 2))]
 
-    def shard_sum(accs):
-        acc = jnp.stack(accs, axis=1)
+    def shard_sum(acc):
         total = acc[0] + sum(shift(acc[T - k], k) for k in range(1, T))
+        return more(total)
+
+    def more(total):
         for bit in range(BITS, row_bits):
             total = total + swap(total, bit)
         return total
@@ -289,19 +308,18 @@
         att_bufs = shards(att_piece)
         small = jnp.concatenate([f32(b_qv).reshape(-1), f32(b_up)])[None]
         for m in tp_bits:
-            small = jnp.concatenate(
-                [small, lax.ppermute(small, "tp", [(i, i ^ m) for i in range(T)])]
-            )
+            other = lax.ppermute(small, "tp", [(i, i ^ m) for i in range(T)])
+            small = jnp.concatenate([small, other])
         up_own = w_up.T.reshape(2, PIECES, FP, D)
         down_own = w_down.reshape(2, PIECES, FP, D)
-        ffn_piece = jnp.stack(
-            [
-                jnp.concatenate([f32(pick(up_own[s], masks[s], 0)), f32(pick(down_own[s], masks[s], 0))])
-                for s in (0, 1)
-            ]
-        )
-        ffn_piece, *att_bufs = lax.optimization_barrier((ffn_piece, *att_bufs))
-        ffn_bufs = shards(ffn_piece)
+        up_piece, down_piece = (
+            jnp.stack([f32(pick(own[s], masks[s], 0)) for s in (0, 1)])
+            for own in (up_own, down_own)
+        )
+        up_piece, down_piece, *att_bufs = lax.optimization_barrier(
+            (up_piece, down_piece, *att_bufs)
+        )
+        up_bufs, down_bufs = shards(up_piece), shards(down_piece)
         shape = (2, quads, T - 1, 2, heads, E, D)
         both = swap_second(swap_first(att_bufs))
         other = swap(both, 0).reshape(shape)
@@ -319,15 +337,20 @@
         )
         bq, bv, bup = bq.reshape(-1), bv.reshape(-1), bup.reshape(-1)
 
+        out_bias, down_bias = f32(b_out), f32(b_down)
+        gain_one, gain_two = f32(gain_attn), f32(gain_ffn)
+        shift_one, shift_two = f32(shift_attn), f32(shift_ffn)
         type_frac = f32(own_slice(type_ids, tokens))[:, None]
         segment = own_slice(segment_ids, nrows)
         table = f32(type_table)
-        embedded = f32(own_slice(features, tokens)) + (table[0] + type_frac * (table[1] - table[0]))
+        embedded = f32(own_slice(features, tokens))
+        embedded = embedded + (table[0] + type_frac * (table[1] - table[0]))
         normal_in = bf16(embedded)
         C = T * width
         H = T * heads
         shape_four = (nrows, length, H, HEAD_DIM)
-        ffn_both = swap_second(swap_first(ffn_bufs))
+        up_both = swap_second(swap_first(up_bufs))
+        down_both = swap_second(swap_first(down_bufs))
         queries = bf16(dot_t(normal_in, wqkv_t[:C]) + bq).reshape(shape_four)
         keys = bf16(dot_t(normal_in, wqkv_t[C : 2 * C])).reshape(shape_four)
         values = bf16(dot_t(normal_in, wqkv_t[2 * C :]) + bv).reshape(shape_four)
@@ -342,24 +365,21 @@
         attended = bf16(
             jnp.einsum("rhqk,rkhd->rqhd", weights, values, preferred_element_type=jnp.float32)
         ).reshape(tokens, C)
-        ffn_other = swap(ffn_both, 0)
-        shape = (2, quads, T - 1, 2, FP, D)
+        shape = (2, quads, T - 1, 1, FP, D)
         up_t, down = (
-            join_ffn(masks_v, own, ffn_both.reshape(shape), ffn_other.reshape(shape), i).reshape(-1, D)
-            for i, own in enumerate((up_own, down_own))
-        )
-        attn_out = dot_n(attended, wo) + f32(b_out)
+            join_ffn(masks_v, own, both.reshape(shape), swap(both, 0).reshape(shape)).reshape(-1, D)
+            for own, both in ((up_own, up_both), (down_own, down_both))
+        )
+        attn_out = dot_n(attended, wo) + out_bias
         normed_a, inverse_a = normalize(embedded + attn_out)
-        gain_one = f32(gain_attn)
-        normed_one = normed_a * gain_one + f32(shift_attn)
+        normed_one = normed_a * gain_one + shift_one
         ffn_in = bf16(normed_one)
         pre_act = dot_t(ffn_in, up_t) + bup
         cdf = 0.5 * (1.0 + lax.erf(pre_act * (0.5**0.5)))
         activated = bf16(pre_act * cdf)
-        ffn_out = dot_n(activated, down) + f32(b_down)
+        ffn_out = dot_n(activated, down) + down_bias
         normed_b, inverse_b = normalize(normed_one + ffn_out)
-        gain_two = f32(gain_ffn)
-        out_own = normed_b * gain_two + f32(shift_ffn)
+        out_own = normed_b * gain_two + shift_two
         gathered_out = lax.all_gather(out_own, "tp", axis=0, tiled=True)
         output = rounded(gathered_out)
 
@@ -383,7 +403,7 @@
         gu_keep = dot_a(grad_pre[:, :half], ffn_in).reshape(six)
         gu = halve_core(gu_keep, gu_send)
         gu = halve_second(halve_first(gu))
-        gf = shard_sum([jnp.concatenate([u, d], axis=1) for u, d in zip(gu, gd)])
+        gf = shard_sum(jnp.stack([jnp.concatenate([u, d], axis=1) for u, d in zip(gu, gd)], axis=1))
         grad_normed = grad_h2 + dot_n(grad_pre, up_t)
         grad_shift_attn = jnp.sum(grad_normed, axis=0)
         grad_gain_attn = jnp.sum(grad_normed * normed_a, axis=0)
@@ -416,7 +436,9 @@
         gq = dot_a(grad_proj, normal_in)
         ga = jnp.concatenate([gq, grad_wo]).reshape(2, 2, T, heads, 2, 2, 2, E, D)
         ga = ga.transpose(4, 0, 5, 6, 2, 1, 3, 7, 8).reshape(2, 2, 2, 2, T, na, D)
-        ga = halve_second(halve_first(halve_core(ga[0], ga[1])))
+        ga = halve_first(halve_core(ga[0], ga[1]))
+        received = [swap(acc[1], bit) for acc, bit in zip(ga, (1, 2))]
+        ga = sum_sets(ga, received)
         ga = shard_sum(ga)
 
         pieces = spread(gf)

time: 713 us -> 669 us (0.938)
  waiting for transfers between devices: 304 us -> 255 us
    ppermute x4 -> x2, starting transfers between devices: 33.3 us -> 3.41 us  [per_device(): other = lax.ppermute(small, 'tp', [(i, i ^ m) for i in range(T)])]
    ppermute x38 -> x43, waiting for transfers between devices: 168 us -> 144 us  [swap(): return lax.ppermute(x, 'rows', [(i, i ^ 1 << bit) for i in range(rows)])]
    ppermute x12 -> x18, starting transfers between devices: 34.7 us -> 55.4 us  [shift(): return lax.ppermute(x, 'tp', [(i, (i + k) % T) for i in range(T)])]
    ppermute x12 -> x18, waiting for transfers between devices: 130 us -> 111 us  [shift(): return lax.ppermute(x, 'tp', [(i, (i + k) % T) for i in range(T)])]
    another operation x10 -> x14, other arithmetic: 22.8 us -> 19.2 us  [swap_second(): jnp.stack([jnp.stack([b, swap(b, bit)]) for b, bit in zip(bufs, (2, 1))])]
    ppermute x38 -> x43, starting transfers between devices: 36 us -> 39.5 us  [swap(): return lax.ppermute(x, 'rows', [(i, i ^ 1 << bit) for i in range(rows)])]
  transfers between devices with their start and end apart: 56 -> 65, of which waited for: 29 -> 26; matrix products, arithmetic and copies ran while one was open for 28% -> 31% of each run, Pallas kernels for 4% -> 5%
where the time goes in v1:
time: 669 us; the launch traced here: 660 us
  waiting for transfers between devices  255 us (38%)
  starting transfers between devices  98.6 us (15%)
  matrix products  86.3 us (13%)
  other arithmetic  85.5 us (13%)
  local copies, waits for them, and re-layouts  73.5 us (11%)
  Pallas kernels  44.7 us (7%)
  between operations  15.9 us (2%)
    ppermute x43, waiting for transfers between devices, swap(): return lax.ppermute(x, 'rows', [(i, i ^ 1 << bit) for i in range(rows)])  144 us
    ppermute x18, waiting for transfers between devices, shift(): return lax.ppermute(x, 'tp', [(i, (i + k) % T) for i in range(T)])  111 us
    ppermute x18, starting transfers between devices, shift(): return lax.ppermute(x, 'tp', [(i, (i + k) % T) for i in range(T)])  55.4 us
    ppermute x43, starting transfers between devices, swap(): return lax.ppermute(x, 'rows', [(i, i ^ 1 << bit) for i in range(rows)])  39.5 us
    dot_general x6, matrix products, dot_a(): lax.dot_general(a, b, (((0,), (0,)), ((), ())), preferred_element_type=jn...  23 us
    dot_general x6, matrix products, dot_t(): lax.dot_general(a, b, (((1,), (1,)), ((), ())), preferred_element_type=jn...  20.9 us
    another operation x14, other arithmetic, swap_second(): jnp.stack([jnp.stack([b, swap(b, bit)]) for b, bit in zip(bufs, (2, 1))])  19.2 us
    dot_general x1, matrix products, per_device(): jnp.einsum('rqhd,rkhd->rhqk', grad_att, values, preferred_element_type=jn...  13.9 us
  transfers between devices with their start and end apart: 65, of which 26 were waited for; matrix products, arithmetic and copies ran while one was open for 31% of the time, Pallas kernels for 5%

profile of v1, /device:TPU:0, one launch (start us, length us, event | category | flops | bytes accessed | tf_op | source)
XLA Modules:
  0.0 659.9 jit_solution(5417407743433978161)
XLA Ops:
  30.0 6.3 collective-permute-done.1
  43.5 5.8 collective-permute-start.18
  53.0 4.4 collective-permute-start.20
  60.9 9.2 %collective-permute-done.19 = f32[2,48,768]{2,1,0:T(8,128)S(1)} collective-permute-done((f32[2,48,768]{2,1,0:T(8,128)S(1)}, f32[2,48,768]{2,1,0:T(8,128)S(1)}, u32[]{:S(2)}, u32[]{:S(2)}) %collective-permute-start.19) | collective-permute-done | bytes 294944 | tf_op jit(solution)/shard_map/ppermute | solution.py:234
  70.1 5.2 collective-permute-start.10
  75.4 3.4 collective-permute-start.11
  82.5 3.8 collective-permute-done.10
  86.4 10.3 %collective-permute-done.11 = f32[2,48,768]{2,1,0:T(8,128)S(1)} collective-permute-done((f32[2,48,768]{2,1,0:T(8,128)}, f32[2,48,768]{2,1,0:T(8,128)S(1)}, u32[]{:S(2)}, u32[]{:S(2)}) %collective-permute-start.11) | collective-permute-done | bytes 294944 | tf_op jit(solution)/shard_map/ppermute | solution.py:234
  101.0 8.7 %collective-permute-done.23 = f32[3,48,768]{2,1,0:T(8,128)S(1)} collective-permute-done((f32[3,48,768]{2,1,0:T(8,128)S(1)}, f32[3,48,768]{2,1,0:T(8,128)S(1)}, u32[]{:S(2)}, u32[]{:S(2)}) %collective-permute-start.23) | collective-permute-done | bytes 442400 | tf_op jit(solution)/shard_map/ppermute | solution.py:231
  134.6 3.6 collective-permute-done.22
  143.5 12.7 %collective-permute-done.14 = f32[2,3,48,768]{3,2,1,0:T(8,128)} collective-permute-done((f32[2,3,48,768]{3,2,1,0:T(8,128)}, f32[2,3,48,768]{3,2,1,0:T(8,128)}, u32[]{:S(2)}, u32[]{:S(2)}) %collective-permute-start.14) | collective-permute-done | bytes 884768 | tf_op jit(solution)/shard_map/ppermute | solution.py:231
  165.4 7.1 %shard_map.280 = bf16[2,2,4,3,64,768]{5,4,3,2,1,0:T(8,128)(2,1)} custom-call(s32[3]{0:T(128)} %pad_add_fusion.masks_ref.scalars_ref, f32[2,2,3,8,8,768]{5,4,3,2,1,0:T(8,128)} %bitcast.280, f32[2,4,3,2,3,8,768]{6,5,4,3,2,1,0:T(8,128)} %pad_maximum_fusion.1.mine_ref, f32[2,4,3,2,3,8,768]{6,5,4,3,2,1,0:T(8,128)} %bitcast.27.other_ref), custom_call_target="tpu_custom_call" | custom-call | tf_op jit(solution)/shard_map/pallas_call | solution.py:169
  187.6 6.9 %fusion.37 = bf16[12,64,512]{2,1,0:T(8,128)(2,1)S(1)} fusion(bf16[512,12,64]{0,2,1:T(8,128)(2,1)S(1)} %bitcast.308, f32[12,512]{1,0:T(8,128)S(1)} %fusion, f32[12,512]{1,0:T(8,128)S(1)} %get-tuple-element.156, f32[12,512,512]{1,2,0:T(8,128)} %copy-done.2, pred[512,512]{0,1:T(8,128)(4,1)S(1)} %copy-done.11), kind=kOutput, calls=%fused_computation.94 | convolution fusion | flops 418775040 | bytes 14467072 | tf_op jit(solution)/shard_map/rhqk,rkhd->rqhd/dot_general | solution.py:366
  197.8 5.8 shard_map.283
  203.6 6.3 shard_map.282
  210.0 5.5 multiply_convert_fusion.1
  221.9 5.3 convert_reduce_fusion
  227.2 3.6 multiply_reduce_fusion.1
  238.6 13.9 %multiply_reduce_fusion = (f32[12,512]{1,0:T(8,128)S(1)}, f32[12,512,512]{1,2,0:T(8,128)}) fusion(f32[12,512]{1,0:T(8,128)S(1)} %log_add_fusion, f32[12,512,512]{1,2,0:T(8,128)} %copy-done.2, pred[512,512]{0,1:T(8,128)(4,1)S(1)} %copy-done.11, bf16[512,12,64]{0,2,1:T(8,128)(2,1)} %bitcast.310, bf16[512,12,64]{0,2,1:T(8,128)(2,1)} %bitcast.309), kind=kOutput, calls=%fused_computation.1 | convolution fusion | flops 418375680 | bytes 27049984 | tf_op jit(solution)/shard_map/rqhd,rkhd->rhqk/dot_general | solution.py:417
  252.5 7.0 %multiply_convert_fusion = bf16[12,512,512]{1,2,0:T(8,128)(2,1)S(1)} fusion(f32[12,512,512]{1,2,0:T(8,128)} %get-tuple-element.166, f32[12,512]{1,0:T(8,128)S(1)} %get-tuple-element.165, f32[12,512]{1,0:T(8,128)S(1)} %log_add_fusion, f32[12,512,512]{1,2,0:T(8,128)S(1)} %bitcast.264, pred[512,512]{0,1:T(8,128)(4,1)S(1)} %copy-done.11), kind=kLoop, calls=%fused_computation | loop fusion | flops 18874368 | bytes 31768576 | tf_op jit(solution)/shard_map/convert_element_type | solution.py:35
  265.0 4.0 convert_reduce_fusion.2
  268.9 6.5 fusion.51
  275.4 7.9 %pad_maximum_fusion = f32[3072,768]{1,0:T(8,128)} fusion(f32[768,768]{1,0:T(8,128)} %fusion.64, f32[2304,768]{1,0:T(8,128)} %fusion.51), kind=kLoop, calls=%fused_computation.9 | loop fusion | flops 2359296 | bytes 18874368 | tf_op jit(solution)/shard_map/concatenate | solution.py:437
  283.4 5.1 copy.69
  288.5 4.5 fusion.106
  293.5 3.7 fusion.26
  297.3 3.7 fusion.22
  304.9 4.4 add.291
  314.3 3.7 fusion.24
  331.6 10.3 %collective-permute-done.51 = f32[2,4,48,768]{3,2,1,0:T(8,128)} collective-permute-done((f32[2,4,48,768]{3,2,1,0:T(8,128)}, f32[2,4,48,768]{3,2,1,0:T(8,128)}, u32[]{:S(2)}, u32[]{:S(2)}) %collective-permute-start.51) | collective-permute-done | bytes 1179680 | tf_op jit(solution)/shard_map/ppermute | solution.py:231
  346.1 21.0 %collective-permute-done.33 = f32[2,4,48,768]{3,2,1,0:T(8,128)S(1)} collective-permute-done((f32[2,4,48,768]{3,2,1,0:T(8,128)S(1)}, f32[2,4,48,768]{3,2,1,0:T(8,128)S(1)}, u32[]{:S(2)}, u32[]{:S(2)}) %collective-permute-start.33) | collective-permute-done | bytes 1179680 | tf_op jit(solution)/shard_map/ppermute | solution.py:231
  369.5 22.8 %collective-permute-done.36 = f32[2,4,48,768]{3,2,1,0:T(8,128)S(1)} collective-permute-done((f32[2,4,48,768]{3,2,1,0:T(8,128)S(1)}, f32[2,4,48,768]{3,2,1,0:T(8,128)S(1)}, u32[]{:S(2)}, u32[]{:S(2)}) %collective-permute-start.36) | collective-permute-done | bytes 1179680 | tf_op jit(solution)/shard_map/ppermute | solution.py:231
  395.8 21.9 %collective-permute-done.39 = f32[4,48,768]{2,1,0:T(8,128)S(1)} collective-permute-done((f32[4,48,768]{2,1,0:T(8,128)S(1)}, f32[4,48,768]{2,1,0:T(8,128)S(1)}, u32[]{:S(2)}, u32[]{:S(2)}) %collective-permute-start.39) | collective-permute-done | bytes 589856 | tf_op jit(solution)/shard_map/ppermute | solution.py:231
  418.5 10.8 %collective-permute-done.41 = f32[4,48,768]{2,1,0:T(8,128)S(1)} collective-permute-done((f32[4,48,768]{2,1,0:T(8,128)S(1)}, f32[4,48,768]{2,1,0:T(8,128)S(1)}, u32[]{:S(2)}, u32[]{:S(2)}) %collective-permute-start.41) | collective-permute-done | bytes 589856 | tf_op jit(solution)/shard_map/ppermute | solution.py:231
  434.6 3.4 collective-permute-start.43
  444.0 20.4 %collective-permute-done.42 = f32[2,96,768]{2,1,0:T(8,128)S(1)} collective-permute-done((f32[2,96,768]{2,1,0:T(8,128)}, f32[2,96,768]{2,1,0:T(8,128)S(1)}, u32[]{:S(2)}, u32[]{:S(2)}) %collective-permute-start.42) | collective-permute-done | bytes 589856 | tf_op jit(solution)/shard_map/ppermute | solution.py:234
  464.4 12.0 %collective-permute-start.57 = (f32[2,48,768]{2,1,0:T(8,128)S(1)}, f32[2,48,768]{2,1,0:T(8,128)S(1)}, u32[]{:S(2)}, u32[]{:S(2)}) collective-permute-start(f32[2,48,768]{2,1,0:T(8,128)S(1)} %get-tuple-element.92), channel_id=1, source_target_pairs={{0,3},{1,0},{2,1},{3,2},{4,7},{5,4},{6,5},{7,6},{8,11},{9,8},{10,9... | collective-permute-start | bytes 884744 | tf_op jit(solution)/shard_map/ppermute | solution.py:234
  476.4 26.4 %collective-permute-done.43 = f32[2,96,768]{2,1,0:T(8,128)S(1)} collective-permute-done((f32[2,96,768]{2,1,0:T(8,128)}, f32[2,96,768]{2,1,0:T(8,128)S(1)}, u32[]{:S(2)}, u32[]{:S(2)}) %collective-permute-start.43) | collective-permute-done | bytes 589856 | tf_op jit(solution)/shard_map/ppermute | solution.py:234
  508.6 5.6 collective-permute-done.55
  514.2 24.3 %collective-permute-done.56 = f32[2,48,768]{2,1,0:T(8,128)S(1)} collective-permute-done((f32[2,48,768]{2,1,0:T(8,128)S(1)}, f32[2,48,768]{2,1,0:T(8,128)S(1)}, u32[]{:S(2)}, u32[]{:S(2)}) %collective-permute-start.56) | collective-permute-done | bytes 294944 | tf_op jit(solution)/shard_map/ppermute | solution.py:234
  544.0 15.5 %collective-permute-done.58 = f32[48,768]{1,0:T(8,128)S(1)} collective-permute-done((f32[48,768]{1,0:T(8,128)S(1)}, f32[48,768]{1,0:T(8,128)S(1)}, u32[]{:S(2)}, u32[]{:S(2)}) %collective-permute-start.58) | collective-permute-done | bytes 147488 | tf_op jit(solution)/shard_map/ppermute | solution.py:231
  562.3 5.3 collective-permute-done.59
  589.9 6.9 %collective-permute-start.26 = (f32[14,768]{1,0:T(8,128)}, f32[14,768]{1,0:T(8,128)S(1)}, u32[]{:S(2)}, u32[]{:S(2)}) collective-permute-start(f32[14,768]{1,0:T(8,128)} %shard_map.286), channel_id=1, source_target_pairs={{0,1},{1,2},{2,3},{3,0},{4,5},{5,6},{6,7},{7,4},{8,9},{9,10},{10,1... | collective-permute-start | bytes 129032 | tf_op jit(solution)/shard_map/ppermute | solution.py:234
  624.3 3.4 shard_map.290
  631.8 5.0 shard_map.284.refs_1_
  636.7 4.7 shard_map.287.refs_2_
  641.4 4.2 fusion.107
  647.6 5.0 shard_map.288
  (421 shorter events, 236.5 us)
Async XLA Ops:
  7.2 624.6 %all-gather.3.cloned.1.call-start = ((), (), s32[]{:S(2)}) async-start(), calls=%async_computation | async-start | bytes 7864320 | tf_op jit(solution)/shard_map/all_gather | solution.py:383
  11.2 17.8 %collective-permute-start = (f32[2,48,768]{2,1,0:T(8,128)}, f32[2,48,768]{2,1,0:T(8,128)}, u32[]{:S(2)}, u32[]{:S(2)}) collective-permute-start(f32[2,48,768]{2,1,0:T(8,128)} %pad_maximum_fusion.38), channel_id=1, source_target_pairs={{0,1},{1,2},{2,3},{3,0},{4,5},{5,6},{6,7},{7,4},{8,9},{9,10},{10,1... | collective-permute-start | bytes 884744 | tf_op jit(solution)/shard_map/ppermute | solution.py:234
  14.3 22.1 %collective-permute-start.1 = (f32[2,48,768]{2,1,0:T(8,128)}, f32[2,48,768]{2,1,0:T(8,128)}, u32[]{:S(2)}, u32[]{:S(2)}) collective-permute-start(f32[2,48,768]{2,1,0:T(8,128)} %pad_maximum_fusion.38), channel_id=1, source_target_pairs={{0,2},{1,3},{2,0},{3,1},{4,6},{5,7},{6,4},{7,5},{8,10},{9,11},{10,... | collective-permute-start | bytes 884744 | tf_op jit(solution)/shard_map/ppermute | solution.py:234
  16.9 20.5 %collective-permute-start.2 = (f32[2,48,768]{2,1,0:T(8,128)}, f32[2,48,768]{2,1,0:T(8,128)}, u32[]{:S(2)}, u32[]{:S(2)}) collective-permute-start(f32[2,48,768]{2,1,0:T(8,128)} %pad_maximum_fusion.38), channel_id=1, source_target_pairs={{0,3},{1,0},{2,1},{3,2},{4,7},{5,4},{6,5},{7,6},{8,11},{9,8},{10,9... | collective-permute-start | bytes 884744 | tf_op jit(solution)/shard_map/ppermute | solution.py:234
  18.3 31.0 %collective-permute-start.8 = (f32[1,1152]{1,0:T(1,128)S(1)}, f32[1,1152]{1,0:T(1,128)}, u32[]{:S(2)}, u32[]{:S(2)}) collective-permute-start(f32[1,1152]{1,0:T(1,128)S(1)} %reshape.460), channel_id=1, source_target_pairs={{0,1},{1,0},{2,3},{3,2},{4,5},{5,4},{6,7},{7,6},{8,9},{9,8},{10,11... | collective-permute-start | bytes 13832 | tf_op jit(solution)/shard_map/ppermute | solution.py:311
  50.0 61.6 %collective-permute-start.9 = (f32[2,1152]{1,0:T(2,128)S(1)}, f32[2,1152]{1,0:T(2,128)S(1)}, u32[]{:S(2)}, u32[]{:S(2)}) collective-permute-start(f32[2,1152]{1,0:T(2,128)S(1)} %pad_maximum_fusion.43), channel_id=1, source_target_pairs={{0,2},{1,3},{2,0},{3,1},{4,6},{5,7},{6,4},{7,5},{8,10},{9,11},{10,... | collective-permute-start | bytes 27656 | tf_op jit(solution)/shard_map/ppermute | solution.py:311
  52.7 17.4 %collective-permute-start.19 = (f32[2,48,768]{2,1,0:T(8,128)S(1)}, f32[2,48,768]{2,1,0:T(8,128)S(1)}, u32[]{:S(2)}, u32[]{:S(2)}) collective-permute-start(f32[2,48,768]{2,1,0:T(8,128)S(1)} %maximum_convert_fusion.1), channel_id=1, source_target_pairs={{0,2},{1,3},{2,0},{3,1},{4,6},{5,7},{6,4},{7,5},{8,10},{9,11},{10,... | collective-permute-start | bytes 884744 | tf_op jit(solution)/shard_map/ppermute | solution.py:234
  53.0 22.4 %collective-permute-start.20 = (f32[2,48,768]{2,1,0:T(8,128)S(1)}, f32[2,48,768]{2,1,0:T(8,128)S(1)}, u32[]{:S(2)}, u32[]{:S(2)}) collective-permute-start(f32[2,48,768]{2,1,0:T(8,128)S(1)} %maximum_convert_fusion.1), channel_id=1, source_target_pairs={{0,3},{1,0},{2,1},{3,2},{4,7},{5,4},{6,5},{7,6},{8,11},{9,8},{10,9... | collective-permute-start | bytes 884744 | tf_op jit(solution)/shard_map/ppermute | solution.py:234
  57.6 21.3 %collective-permute-start.4 = (f32[2,3,48,768]{3,2,1,0:T(8,128)S(1)}, f32[2,3,48,768]{3,2,1,0:T(8,128)S(1)}, u32[]{:S(2)}, u32[]{:S(2)}) collective-permute-start(f32[2,3,48,768]{3,2,1,0:T(8,128)S(1)} %get-tuple-element.107), channel_id=1, source_target_pairs={{0,16},{4,20},{8,24},{12,28},{16,0},{20,4},{24,8},{28,12},{1,17},{... | collective-permute-start | bytes 2654216 | tf_op jit(solution)/shard_map/ppermute | solution.py:231
  59.3 20.3 %collective-permute-start.6 = (f32[2,3,48,768]{3,2,1,0:T(8,128)S(1)}, f32[2,3,48,768]{3,2,1,0:T(8,128)S(1)}, u32[]{:S(2)}, u32[]{:S(2)}) collective-permute-start(f32[2,3,48,768]{3,2,1,0:T(8,128)S(1)} %get-tuple-element.109), channel_id=1, source_target_pairs={{0,8},{4,12},{8,0},{12,4},{16,24},{20,28},{24,16},{28,20},{1,9},{5... | collective-permute-start | bytes 2654216 | tf_op jit(solution)/shard_map/ppermute | solution.py:231
  75.4 21.3 %collective-permute-start.11 = (f32[2,48,768]{2,1,0:T(8,128)}, f32[2,48,768]{2,1,0:T(8,128)S(1)}, u32[]{:S(2)}, u32[]{:S(2)}) collective-permute-start(f32[2,48,768]{2,1,0:T(8,128)} %maximum_convert_fusion), channel_id=1, source_target_pairs={{0,2},{1,3},{2,0},{3,1},{4,6},{5,7},{6,4},{7,5},{8,10},{9,11},{10,... | collective-permute-start | bytes 884744 | tf_op jit(solution)/shard_map/ppermute | solution.py:234
  78.9 18.3 %collective-permute-start.12 = (f32[2,48,768]{2,1,0:T(8,128)}, f32[2,48,768]{2,1,0:T(8,128)S(1)}, u32[]{:S(2)}, u32[]{:S(2)}) collective-permute-start(f32[2,48,768]{2,1,0:T(8,128)} %maximum_convert_fusion), channel_id=1, source_target_pairs={{0,3},{1,0},{2,1},{3,2},{4,7},{5,4},{6,5},{7,6},{8,11},{9,8},{10,9... | collective-permute-start | bytes 884744 | tf_op jit(solution)/shard_map/ppermute | solution.py:234
  79.6 18.3 %collective-permute-start.21 = (f32[3,48,768]{2,1,0:T(8,128)S(1)}, f32[3,48,768]{2,1,0:T(8,128)S(1)}, u32[]{:S(2)}, u32[]{:S(2)}) collective-permute-start(f32[3,48,768]{2,1,0:T(8,128)S(1)} %get-tuple-element.119), channel_id=1, source_target_pairs={{0,8},{4,12},{8,0},{12,4},{16,24},{20,28},{24,16},{28,20},{1,9},{5... | collective-permute-start | bytes 1327112 | tf_op jit(solution)/shard_map/ppermute | solution.py:231
  86.3 79.1 %collective-permute-start.7 = (f32[2,2,2,3,48,768]{5,4,3,2,1,0:T(8,128)}, f32[2,2,2,3,48,768]{5,4,3,2,1,0:T(8,128)}, u32[]{:S(2)}, u32[]{:S(2)}) collective-permute-start(f32[2,2,2,3,48,768]{5,4,3,2,1,0:T(8,128)} %pad_maximum_fusion.2), channel_id=1, source_target_pairs={{0,4},{4,0},{8,12},{12,8},{16,20},{20,16},{24,28},{28,24},{1,5},{5... | collective-permute-start | bytes 10616840 | tf_op jit(solution)/shard_map/ppermute | solution.py:231
  97.3 19.1 %collective-permute-start.13 = (f32[3,48,768]{2,1,0:T(8,128)S(1)}, f32[3,48,768]{2,1,0:T(8,128)S(1)}, u32[]{:S(2)}, u32[]{:S(2)}) collective-permute-start(f32[3,48,768]{2,1,0:T(8,128)S(1)} %get-tuple-element.123), channel_id=1, source_target_pairs={{0,8},{4,12},{8,0},{12,4},{16,24},{20,28},{24,16},{28,20},{1,9},{5... | collective-permute-start | bytes 1327112 | tf_op jit(solution)/shard_map/ppermute | solution.py:231
  98.0 21.3 %collective-permute-start.15 = (f32[3,48,768]{2,1,0:T(8,128)S(1)}, f32[3,48,768]{2,1,0:T(8,128)S(1)}, u32[]{:S(2)}, u32[]{:S(2)}) collective-permute-start(f32[3,48,768]{2,1,0:T(8,128)S(1)} %get-tuple-element.125), channel_id=1, source_target_pairs={{0,16},{4,20},{8,24},{12,28},{16,0},{20,4},{24,8},{28,12},{1,17},{... | collective-permute-start | bytes 1327112 | tf_op jit(solution)/shard_map/ppermute | solution.py:231
  109.7 28.5 %collective-permute-start.22 = (f32[2,3,48,768]{3,2,1,0:T(8,128)}, f32[2,3,48,768]{3,2,1,0:T(8,128)}, u32[]{:S(2)}, u32[]{:S(2)}) collective-permute-start(f32[2,3,48,768]{3,2,1,0:T(8,128)} %get-tuple-element.99), channel_id=1, source_target_pairs={{0,16},{4,20},{8,24},{12,28},{16,0},{20,4},{24,8},{28,12},{1,17},{... | collective-permute-start | bytes 2654216 | tf_op jit(solution)/shard_map/ppermute | solution.py:231
  111.6 28.3 %collective-permute-start.24 = (f32[2,3,48,768]{3,2,1,0:T(8,128)}, f32[2,3,48,768]{3,2,1,0:T(8,128)}, u32[]{:S(2)}, u32[]{:S(2)}) collective-permute-start(f32[2,3,48,768]{3,2,1,0:T(8,128)} %get-tuple-element.101), channel_id=1, source_target_pairs={{0,8},{4,12},{8,0},{12,4},{16,24},{20,28},{24,16},{28,20},{1,9},{5... | collective-permute-start | bytes 2654216 | tf_op jit(solution)/shard_map/ppermute | solution.py:231
  117.8 38.4 %collective-permute-start.14 = (f32[2,3,48,768]{3,2,1,0:T(8,128)}, f32[2,3,48,768]{3,2,1,0:T(8,128)}, u32[]{:S(2)}, u32[]{:S(2)}) collective-permute-start(f32[2,3,48,768]{3,2,1,0:T(8,128)} %get-tuple-element.103), channel_id=1, source_target_pairs={{0,16},{4,20},{8,24},{12,28},{16,0},{20,4},{24,8},{28,12},{1,17},{... | collective-permute-start | bytes 2654216 | tf_op jit(solution)/shard_map/ppermute | solution.py:231
  120.6 37.2 %collective-permute-start.16 = (f32[2,3,48,768]{3,2,1,0:T(8,128)}, f32[2,3,48,768]{3,2,1,0:T(8,128)}, u32[]{:S(2)}, u32[]{:S(2)}) collective-permute-start(f32[2,3,48,768]{3,2,1,0:T(8,128)} %get-tuple-element.105), channel_id=1, source_target_pairs={{0,8},{4,12},{8,0},{12,4},{16,24},{20,28},{24,16},{28,20},{1,9},{5... | collective-permute-start | bytes 2654216 | tf_op jit(solution)/shard_map/ppermute | solution.py:231
  143.5 54.3 %collective-permute-start.25 = (f32[2,2,2,3,48,768]{5,4,3,2,1,0:T(8,128)}, f32[2,2,2,3,48,768]{5,4,3,2,1,0:T(8,128)}, u32[]{:S(2)}, u32[]{:S(2)}) collective-permute-start(f32[2,2,2,3,48,768]{5,4,3,2,1,0:T(8,128)} %pad_maximum_fusion.6), channel_id=1, source_target_pairs={{0,4},{4,0},{8,12},{12,8},{16,20},{20,16},{24,28},{28,24},{1,5},{5... | collective-permute-start | bytes 10616840 | tf_op jit(solution)/shard_map/ppermute | solution.py:231
  161.4 42.2 %collective-permute-start.17 = (f32[2,2,2,3,48,768]{5,4,3,2,1,0:T(8,128)}, f32[2,2,2,3,48,768]{5,4,3,2,1,0:T(8,128)}, u32[]{:S(2)}, u32[]{:S(2)}) collective-permute-start(f32[2,2,2,3,48,768]{5,4,3,2,1,0:T(8,128)} %pad_maximum_fusion.4), channel_id=1, source_target_pairs={{0,4},{4,0},{8,12},{12,8},{16,20},{20,16},{24,28},{28,24},{1,5},{5... | collective-permute-start | bytes 10616840 | tf_op jit(solution)/shard_map/ppermute | solution.py:231
  238.3 409.3 %all-gather.5.cloned.1.call-start = ((), (), s32[]{:S(2)}) async-start(), calls=%async_computation.1 | async-start | bytes 7864320 | tf_op jit(solution)/shard_map/all_gather | solution.py:435
  297.2 24.0 %collective-permute-start.32 = (f32[2,2,2,4,48,768]{5,4,3,2,1,0:T(8,128)}, f32[2,2,2,4,48,768]{5,4,3,2,1,0:T(8,128)}, u32[]{:S(2)}, u32[]{:S(2)}) collective-permute-start(f32[2,2,2,4,48,768]{5,4,3,2,1,0:T(8,128)} %bitcast.79), channel_id=1, source_target_pairs={{0,4},{4,0},{8,12},{12,8},{16,20},{20,16},{24,28},{28,24},{1,5},{5... | collective-permute-start | bytes 14155784 | tf_op jit(solution)/shard_map/ppermute | solution.py:231
  301.0 26.3 %collective-permute-start.35 = (f32[2,2,2,4,48,768]{5,4,3,2,1,0:T(8,128)}, f32[2,2,2,4,48,768]{5,4,3,2,1,0:T(8,128)}, u32[]{:S(2)}, u32[]{:S(2)}) collective-permute-start(f32[2,2,2,4,48,768]{5,4,3,2,1,0:T(8,128)} %bitcast.85), channel_id=1, source_target_pairs={{0,4},{4,0},{8,12},{12,8},{16,20},{20,16},{24,28},{28,24},{1,5},{5... | collective-permute-start | bytes 14155784 | tf_op jit(solution)/shard_map/ppermute | solution.py:231
  312.7 29.2 %collective-permute-start.51 = (f32[2,4,48,768]{3,2,1,0:T(8,128)}, f32[2,4,48,768]{3,2,1,0:T(8,128)}, u32[]{:S(2)}, u32[]{:S(2)}) collective-permute-start(f32[2,4,48,768]{3,2,1,0:T(8,128)} %get-tuple-element.64), channel_id=1, source_target_pairs={{0,16},{4,20},{8,24},{12,28},{16,0},{20,4},{24,8},{28,12},{1,17},{... | collective-permute-start | bytes 3538952 | tf_op jit(solution)/shard_map/ppermute | solution.py:231
  313.5 29.2 %collective-permute-start.53 = (f32[2,4,48,768]{3,2,1,0:T(8,128)}, f32[2,4,48,768]{3,2,1,0:T(8,128)}, u32[]{:S(2)}, u32[]{:S(2)}) collective-permute-start(f32[2,4,48,768]{3,2,1,0:T(8,128)} %get-tuple-element.63), channel_id=1, source_target_pairs={{0,8},{4,12},{8,0},{12,4},{16,24},{20,28},{24,16},{28,20},{1,9},{5... | collective-permute-start | bytes 3538952 | tf_op jit(solution)/shard_map/ppermute | solution.py:231
  324.8 42.3 %collective-permute-start.33 = (f32[2,4,48,768]{3,2,1,0:T(8,128)S(1)}, f32[2,4,48,768]{3,2,1,0:T(8,128)S(1)}, u32[]{:S(2)}, u32[]{:S(2)}) collective-permute-start(f32[2,4,48,768]{3,2,1,0:T(8,128)S(1)} %get-tuple-element.68), channel_id=1, source_target_pairs={{0,16},{4,20},{8,24},{12,28},{16,0},{20,4},{24,8},{28,12},{1,17},{... | collective-permute-start | bytes 3538952 | tf_op jit(solution)/shard_map/ppermute | solution.py:231
  326.1 41.8 %collective-permute-start.38 = (f32[2,4,48,768]{3,2,1,0:T(8,128)S(1)}, f32[2,4,48,768]{3,2,1,0:T(8,128)S(1)}, u32[]{:S(2)}, u32[]{:S(2)}) collective-permute-start(f32[2,4,48,768]{3,2,1,0:T(8,128)S(1)} %get-tuple-element.67), channel_id=1, source_target_pairs={{0,8},{4,12},{8,0},{12,4},{16,24},{20,28},{24,16},{28,20},{1,9},{5... | collective-permute-start | bytes 3538952 | tf_op jit(solution)/shard_map/ppermute | solution.py:231
  330.7 61.7 %collective-permute-start.36 = (f32[2,4,48,768]{3,2,1,0:T(8,128)S(1)}, f32[2,4,48,768]{3,2,1,0:T(8,128)S(1)}, u32[]{:S(2)}, u32[]{:S(2)}) collective-permute-start(f32[2,4,48,768]{3,2,1,0:T(8,128)S(1)} %get-tuple-element.72), channel_id=1, source_target_pairs={{0,16},{4,20},{8,24},{12,28},{16,0},{20,4},{24,8},{28,12},{1,17},{... | collective-permute-start | bytes 3538952 | tf_op jit(solution)/shard_map/ppermute | solution.py:231
  341.9 51.2 %collective-permute-start.40 = (f32[2,4,48,768]{3,2,1,0:T(8,128)S(1)}, f32[2,4,48,768]{3,2,1,0:T(8,128)S(1)}, u32[]{:S(2)}, u32[]{:S(2)}) collective-permute-start(f32[2,4,48,768]{3,2,1,0:T(8,128)S(1)} %get-tuple-element.71), channel_id=1, source_target_pairs={{0,8},{4,12},{8,0},{12,4},{16,24},{20,28},{24,16},{28,20},{1,9},{5... | collective-permute-start | bytes 3538952 | tf_op jit(solution)/shard_map/ppermute | solution.py:231
  344.7 93.2 %collective-permute-start.52 = (f32[4,48,768]{2,1,0:T(8,128)S(1)}, f32[4,48,768]{2,1,0:T(8,128)}, u32[]{:S(2)}, u32[]{:S(2)}) collective-permute-start(f32[4,48,768]{2,1,0:T(8,128)S(1)} %slice_bitcast_fusion.15), channel_id=1, source_target_pairs={{0,8},{4,12},{8,0},{12,4},{16,24},{20,28},{24,16},{28,20},{1,9},{5... | collective-permute-start | bytes 1769480 | tf_op jit(solution)/shard_map/ppermute | solution.py:231
  367.1 70.9 %collective-permute-start.54 = (f32[4,48,768]{2,1,0:T(8,128)S(1)}, f32[4,48,768]{2,1,0:T(8,128)}, u32[]{:S(2)}, u32[]{:S(2)}) collective-permute-start(f32[4,48,768]{2,1,0:T(8,128)S(1)} %slice_bitcast_fusion.14), channel_id=1, source_target_pairs={{0,16},{4,20},{8,24},{12,28},{16,0},{20,4},{24,8},{28,12},{1,17},{... | collective-permute-start | bytes 1769480 | tf_op jit(solution)/shard_map/ppermute | solution.py:231
  368.2 49.4 %collective-permute-start.39 = (f32[4,48,768]{2,1,0:T(8,128)S(1)}, f32[4,48,768]{2,1,0:T(8,128)S(1)}, u32[]{:S(2)}, u32[]{:S(2)}) collective-permute-start(f32[4,48,768]{2,1,0:T(8,128)S(1)} %slice_bitcast_fusion.18), channel_id=1, source_target_pairs={{0,16},{4,20},{8,24},{12,28},{16,0},{20,4},{24,8},{28,12},{1,17},{... | collective-permute-start | bytes 1769480 | tf_op jit(solution)/shard_map/ppermute | solution.py:231
  393.5 35.8 %collective-permute-start.41 = (f32[4,48,768]{2,1,0:T(8,128)S(1)}, f32[4,48,768]{2,1,0:T(8,128)S(1)}, u32[]{:S(2)}, u32[]{:S(2)}) collective-permute-start(f32[4,48,768]{2,1,0:T(8,128)S(1)} %slice_bitcast_fusion.16), channel_id=1, source_target_pairs={{0,16},{4,20},{8,24},{12,28},{16,0},{20,4},{24,8},{28,12},{1,17},{... | collective-permute-start | bytes 1769480 | tf_op jit(solution)/shard_map/ppermute | solution.py:231
  394.9 34.6 %collective-permute-start.34 = (f32[4,48,768]{2,1,0:T(8,128)S(1)}, f32[4,48,768]{2,1,0:T(8,128)S(1)}, u32[]{:S(2)}, u32[]{:S(2)}) collective-permute-start(f32[4,48,768]{2,1,0:T(8,128)S(1)} %slice_bitcast_fusion.22), channel_id=1, source_target_pairs={{0,8},{4,12},{8,0},{12,4},{16,24},{20,28},{24,16},{28,20},{1,9},{5... | collective-permute-start | bytes 1769480 | tf_op jit(solution)/shard_map/ppermute | solution.py:231
  432.5 31.9 %collective-permute-start.42 = (f32[2,96,768]{2,1,0:T(8,128)}, f32[2,96,768]{2,1,0:T(8,128)S(1)}, u32[]{:S(2)}, u32[]{:S(2)}) collective-permute-start(f32[2,96,768]{2,1,0:T(8,128)} %get-tuple-element.74), channel_id=1, source_target_pairs={{0,1},{1,2},{2,3},{3,0},{4,5},{5,6},{6,7},{7,4},{8,9},{9,10},{10,1... | collective-permute-start | bytes 1769480 | tf_op jit(solution)/shard_map/ppermute | solution.py:234
  434.6 68.3 %collective-permute-start.43 = (f32[2,96,768]{2,1,0:T(8,128)}, f32[2,96,768]{2,1,0:T(8,128)S(1)}, u32[]{:S(2)}, u32[]{:S(2)}) collective-permute-start(f32[2,96,768]{2,1,0:T(8,128)} %get-tuple-element.73), channel_id=1, source_target_pairs={{0,2},{1,3},{2,0},{3,1},{4,6},{5,7},{6,4},{7,5},{8,10},{9,11},{10,... | collective-permute-start | bytes 1769480 | tf_op jit(solution)/shard_map/ppermute | solution.py:234
  437.9 66.1 %collective-permute-start.44 = (f32[2,96,768]{2,1,0:T(8,128)}, f32[2,96,768]{2,1,0:T(8,128)}, u32[]{:S(2)}, u32[]{:S(2)}) collective-permute-start(f32[2,96,768]{2,1,0:T(8,128)} %get-tuple-element.75), channel_id=1, source_target_pairs={{0,3},{1,0},{2,1},{3,2},{4,7},{5,4},{6,5},{7,6},{8,11},{9,8},{10,9... | collective-permute-start | bytes 1769480 | tf_op jit(solution)/shard_map/ppermute | solution.py:234
  441.9 72.3 %collective-permute-start.55 = (f32[2,48,768]{2,1,0:T(8,128)S(1)}, f32[2,48,768]{2,1,0:T(8,128)S(1)}, u32[]{:S(2)}, u32[]{:S(2)}) collective-permute-start(f32[2,48,768]{2,1,0:T(8,128)S(1)} %get-tuple-element.93), channel_id=1, source_target_pairs={{0,1},{1,2},{2,3},{3,0},{4,5},{5,6},{6,7},{7,4},{8,9},{9,10},{10,1... | collective-permute-start | bytes 884744 | tf_op jit(solution)/shard_map/ppermute | solution.py:234
  444.0 94.5 %collective-permute-start.56 = (f32[2,48,768]{2,1,0:T(8,128)S(1)}, f32[2,48,768]{2,1,0:T(8,128)S(1)}, u32[]{:S(2)}, u32[]{:S(2)}) collective-permute-start(f32[2,48,768]{2,1,0:T(8,128)S(1)} %get-tuple-element.91), channel_id=1, source_target_pairs={{0,2},{1,3},{2,0},{3,1},{4,6},{5,7},{6,4},{7,5},{8,10},{9,11},{10,... | collective-permute-start | bytes 884744 | tf_op jit(solution)/shard_map/ppermute | solution.py:234
  464.4 74.1 %collective-permute-start.57 = (f32[2,48,768]{2,1,0:T(8,128)S(1)}, f32[2,48,768]{2,1,0:T(8,128)S(1)}, u32[]{:S(2)}, u32[]{:S(2)}) collective-permute-start(f32[2,48,768]{2,1,0:T(8,128)S(1)} %get-tuple-element.92), channel_id=1, source_target_pairs={{0,3},{1,0},{2,1},{3,2},{4,7},{5,4},{6,5},{7,6},{8,11},{9,8},{10,9... | collective-permute-start | bytes 884744 | tf_op jit(solution)/shard_map/ppermute | solution.py:234
  505.4 34.1 %collective-permute-start.45 = (f32[96,768]{1,0:T(8,128)S(1)}, f32[96,768]{1,0:T(8,128)S(1)}, u32[]{:S(2)}, u32[]{:S(2)}) collective-permute-start(f32[96,768]{1,0:T(8,128)S(1)} %get-tuple-element.113), channel_id=1, source_target_pairs={{0,8},{4,12},{8,0},{12,4},{16,24},{20,28},{24,16},{28,20},{1,9},{5... | collective-permute-start | bytes 884744 | tf_op jit(solution)/shard_map/ppermute | solution.py:231
  507.1 34.1 %collective-permute-start.47 = (f32[96,768]{1,0:T(8,128)S(1)}, f32[96,768]{1,0:T(8,128)S(1)}, u32[]{:S(2)}, u32[]{:S(2)}) collective-permute-start(f32[96,768]{1,0:T(8,128)S(1)} %get-tuple-element.114), channel_id=1, source_target_pairs={{0,16},{4,20},{8,24},{12,28},{16,0},{20,4},{24,8},{28,12},{1,17},{... | collective-permute-start | bytes 884744 | tf_op jit(solution)/shard_map/ppermute | solution.py:231
  539.6 20.6 %collective-permute-start.46 = (f32[2,96,768]{2,1,0:T(8,128)S(1)}, f32[2,96,768]{2,1,0:T(8,128)S(1)}, u32[]{:S(2)}, u32[]{:S(2)}) collective-permute-start(f32[2,96,768]{2,1,0:T(8,128)S(1)} %get-tuple-element.111), channel_id=1, source_target_pairs={{0,16},{4,20},{8,24},{12,28},{16,0},{20,4},{24,8},{28,12},{1,17},{... | collective-permute-start | bytes 1769480 | tf_op jit(solution)/shard_map/ppermute | solution.py:231
  541.3 19.1 %collective-permute-start.48 = (f32[2,96,768]{2,1,0:T(8,128)S(1)}, f32[2,96,768]{2,1,0:T(8,128)S(1)}, u32[]{:S(2)}, u32[]{:S(2)}) collective-permute-start(f32[2,96,768]{2,1,0:T(8,128)S(1)} %get-tuple-element.117), channel_id=1, source_target_pairs={{0,8},{4,12},{8,0},{12,4},{16,24},{20,28},{24,16},{28,20},{1,9},{5... | collective-permute-start | bytes 1769480 | tf_op jit(solution)/shard_map/ppermute | solution.py:231
  560.6 76.1 %collective-permute-start.49 = (f32[2,4,96,768]{3,2,1,0:T(8,128)S(1)}, f32[2,4,96,768]{3,2,1,0:T(8,128)}, u32[]{:S(2)}, u32[]{:S(2)}) collective-permute-start(f32[2,4,96,768]{3,2,1,0:T(8,128)S(1)} %pad_maximum_fusion.9.mine_ref), channel_id=1, source_target_pairs={{0,4},{4,0},{8,12},{12,8},{16,20},{20,16},{24,28},{28,24},{1,5},{5... | collective-permute-start | bytes 7077896 | tf_op jit(solution)/shard_map/ppermute | solution.py:231
  570.4 53.9 %collective-permute-start.62 = (f32[2,4,48,768]{3,2,1,0:T(8,128)S(1)}, f32[2,4,48,768]{3,2,1,0:T(8,128)}, u32[]{:S(2)}, u32[]{:S(2)}) collective-permute-start(f32[2,4,48,768]{3,2,1,0:T(8,128)S(1)} %pad_maximum_fusion.18.mine_ref), channel_id=1, source_target_pairs={{0,4},{4,0},{8,12},{12,8},{16,20},{20,16},{24,28},{28,24},{1,5},{5... | collective-permute-start | bytes 3538952 | tf_op jit(solution)/shard_map/ppermute | solution.py:231
  (86 other events, 846.7 us)
Sparse Core Ops, SparseCore 0:
  238.4 115.8 all-gather.2
  355.9 167.9 all-gather.4
